TPU v7x, 32 devices: a whole 2x2x4 slice. The times are simulated.
32 devices in a mesh: dp: 2 (over x), row: 4 (over z), col: 4 (over y, core).
Axes of the slice: x: 2, y: 2, z: 4, core: 2. Of those that a mesh axis runs over, the one named last changes fastest.
Arguments:
- block_in: float32 [2048, 1152], P(('dp', 'col'), 'row'), may hold values from -6 to 6
- labels: int32 [2], P('dp'), may hold values from 0 to 1000
- steps_t: int32 [2], P('dp'), may hold values from 0 to 999
- out_cot: float32 [2048, 1152], P(('dp', 'col'), 'row'), may hold values from -6 to 6
- class_table: float32 [1001, 1152], P(None, 'col'), may hold values from -6 to 6
- w_ada: float32 [1152, 6, 1152], P('col', None, 'row'), may hold values from -0.1875 to 0.1875
- b_ada: float32 [6, 1152], P(None, 'row'), may hold values from -3 to 3
- w_qkv: float32 [1152, 3, 1152], P('row', None, 'col'), may hold values from -0.125 to 0.125
- b_qv: float32 [2, 1152], P(None, 'col'), may hold values from -3 to 3
- w_out: float32 [1152, 1152], P('col', 'row'), may hold values from -3.5 to 3.5
- b_out: float32 [1152], P('row'), may hold values from -3 to 3
- w_up: float32 [1152, 4608], P('row', 'col'), may hold values from -0.1875 to 0.1875
- b_up: float32 [4608], P('col'), may hold values from -3 to 3
- w_down: float32 [4608, 1152], P('col', 'row'), may hold values from -0.09375 to 0.09375
- b_down: float32 [1152], P('row'), may hold values from -3 to 3
Outputs:
- block_out: float32 [2048, 1152], P(('dp', 'col'), 'row')
- in_grad: float32 [2048, 1152], P(('dp', 'col'), 'row')
- table_grad: float32 [1001, 1152], P(None, 'col')
- ada_grad: float32 [1152, 6, 1152], P('col', None, 'row')
- ada_bias_grad: float32 [6, 1152], P(None, 'row')
- qkv_grad: float32 [1152, 3, 1152], P('row', None, 'col')
- qv_bias_grad: float32 [2, 1152], P(None, 'col')
- out_grad: float32 [1152, 1152], P('col', 'row')
- out_bias_grad: float32 [1152], P('row')
- up_grad: float32 [1152, 4608], P('row', 'col')
- up_bias_grad: float32 [4608], P('col')
- down_grad: float32 [4608, 1152], P('col', 'row')
- down_bias_grad: float32 [1152], P('row')
All inputs are finite; a program needn't handle non-finite values.
Results may differ from a plain program's by a relative error of at most 0.0003.
Values sent between devices are 32-bit elements; how exact they have to be, the bound alone decides.
No kernel may reach another device: no remote copies, remote signals or barrier semaphores. Data moves between devices by JAX's collectives and lax.ppermute only.
A program may use at most 128 MiB of HBM per device.

v0:
```python
from functools import partial
import math

import jax
import jax.numpy as jnp
from jax import lax
from jax.experimental import pallas as pl
from jax.experimental.layout import Layout, with_layout_constraint
from jax.experimental.pallas import tpu as pltpu
from jax.sharding import PartitionSpec as P


HD = 72
norm_epsilon = 1e-06
fast_mode = lax.Precision.HIGH


def contract(left, right, left_dim, right_dim, precision=fast_mode):
    return lax.dot_general(
        left,
        right,
        (((left_dim,), (right_dim,)), ((), ())),
        precision=precision,
        preferred_element_type=jnp.float32,
    )


def row_major(values):
    return with_layout_constraint(values, Layout(major_to_minor=tuple(range(values.ndim))))


def shift_row(values, step):
    count = lax.axis_size("row")
    if step % count == 0:
        return values
    return lax.ppermute(values, "row", [(i, (i + step) % count) for i in range(count)])


def shift_chip(values, step):
    count = lax.axis_size("col") // 2
    if step % count == 0:
        return values
    pairs = [
        (2 * i + core, 2 * ((i + step) % count) + core) for i in range(count) for core in range(2)
    ]
    return lax.ppermute(values, "col", pairs)


def swap_core(values):
    return lax.ppermute(values, "col", [(i, i ^ 1) for i in range(lax.axis_size("col"))])


def swap_dp(values):
    return lax.ppermute(values, "dp", [(0, 1), (1, 0)])


def butterfly(values, axis):
    count = lax.axis_size(axis)
    step = 1
    while step < count:
        values = values + lax.ppermute(values, axis, [(i, i ^ step) for i in range(count)])
        step *= 2
    return values


def row_order():
    count = lax.axis_size("row")
    return sorted(range(count), key=lambda step: (min(step, count - step), step))


def spread(block, ready=()):
    count = lax.axis_size("row")
    chips = lax.axis_size("col") // 2
    by_step = {0: block}
    own_chips = [shift_chip(block, chip) for chip in range(chips)]
    for step in row_order()[1:-1]:
        if step <= count // 2:
            by_step[step] = shift_row(by_step[step - 1], 1)
        else:
            by_step[step] = shift_row(by_step[(step + 1) % count], -1)
    by_step, ready = lax.optimization_barrier((by_step, ready))
    last = row_order()[-1]
    by_step[last] = shift_row(by_step[last - 1], 1)
    groups = [own_chips]
    for step in row_order()[1:]:
        groups.append([shift_chip(by_step[step], chip) for chip in range(chips)])
    near = jnp.concatenate(sum(groups[:-1], []), axis=0)
    far = jnp.concatenate(groups[-1], axis=0)
    return [near, far, swap_core(near), swap_core(far)], ready


def by_piece(function, pieces):
    return jnp.concatenate([function(piece) for piece in pieces], axis=0)


def scatter_tokens(partial_rows, tokens, fill, fill_row=lambda earlier, value: value):
    count = lax.axis_size("row")
    chips = lax.axis_size("col") // 2
    half = tokens // 2
    group = half // count
    size = group // chips
    split = half - group
    far = swap_core(partial_rows(half + split, group))
    near = swap_core(partial_rows(half, split))
    far = partial_rows(split, group) + far
    near = partial_rows(0, split) + near
    filled = fill(near)
    sums = {}
    for place, step in reversed(list(enumerate(row_order()))):
        part = far if place == count - 1 else near[place * group : (place + 1) * group]
        total = part[:size]
        for chip in range(1, chips):
            total = total + shift_chip(part[chip * size : (chip + 1) * size], -chip)
        sums[step] = total
    filled = fill_row(sums[1], filled)
    for step in reversed(row_order()[1:]):
        if step <= count // 2:
            sums[step - 1] = sums[step - 1] + shift_row(sums[step], -1)
        else:
            back = (step + 1) % count
            sums[back] = sums[back] + shift_row(sums[step], 1)
    return sums[0], filled


def after(values, earlier):
    return lax.optimization_barrier((values, earlier))[0]


def copy_blocks(size, places_ref, source_ref, target_ref):
    def body(block, carry):
        start = pl.multiple_of(places_ref[block] * size, 8)
        target = pl.multiple_of(block * size, 8)
        target_ref[pl.ds(target, size), :] = source_ref[pl.ds(start, size), :]
        return carry

    lax.fori_loop(0, places_ref.shape[0], body, 0)


def take_blocks(values, places):
    size = values.shape[0] // places.shape[0]
    return pl.pallas_call(
        partial(copy_blocks, size),
        in_specs=[
            pl.BlockSpec(memory_space=pltpu.SMEM),
            pl.BlockSpec(memory_space=pltpu.VMEM),
        ],
        out_specs=pl.BlockSpec(memory_space=pltpu.VMEM),
        out_shape=jax.ShapeDtypeStruct(values.shape, values.dtype),
        cost_estimate=pl.CostEstimate(flops=0, transcendentals=0, bytes_accessed=8 * values.size),
        name="take_blocks",
    )(places, values)


def block_places():
    rows, cols = lax.axis_size("row"), lax.axis_size("col")
    chips = cols // 2
    me_row, me_col = lax.axis_index("row"), lax.axis_index("col")
    tokens_mesh = []
    for core in range(2):
        for step in row_order():
            for chip in range(chips):
                col = (me_col // 2 - chip) % chips * 2 + (me_col % 2 + core) % 2
                tokens_mesh.append(col * rows + (me_row - step) % rows)
    tokens_mesh = jnp.stack(tokens_mesh).astype(jnp.int32)
    numbers = jnp.arange(rows * cols, dtype=jnp.int32)
    mesh_tokens = jnp.sum(
        jnp.where(tokens_mesh[None, :] == numbers[:, None], numbers[None, :], 0), axis=1
    )
    return tokens_mesh, mesh_tokens


def gather_mesh(local):
    return lax.all_gather(local, ("col", "row"), axis=0, tiled=True)


def scatter_mesh(partial_sums):
    return lax.psum_scatter(partial_sums, ("col", "row"), scatter_dimension=0, tiled=True)


def row_outgoing(blocks):
    count = lax.axis_size("row")
    me = lax.axis_index("row")
    return [
        lax.dynamic_index_in_dim(blocks, (me + step) % count, 0, keepdims=False)
        for step in range(count)
    ]


def row_send(outgoing):
    return [shift_row(block, step) for step, block in enumerate(outgoing)]


def row_parts(blocks):
    return row_send(row_outgoing(blocks))


def by_source(parts):
    count = lax.axis_size("row")
    me = lax.axis_index("row")
    stacked = jnp.stack(parts)
    return [
        lax.dynamic_index_in_dim(stacked, (me - row) % count, 0, keepdims=False)
        for row in range(count)
    ]


def move_rows(blocks):
    return row_major(jnp.stack(row_parts(row_major(blocks))))


def own_half(blocks, axis):
    if lax.axis_size("dp") != 2:
        return blocks
    half = blocks.shape[axis] // 2
    return lax.dynamic_slice_in_dim(blocks, lax.axis_index("dp") * half, half, axis)


def share_blocks(mine):
    if lax.axis_size("dp") != 2:
        return mine[None]
    return jnp.stack([mine, swap_dp(mine)])


def order_blocks(both):
    if lax.axis_size("dp") != 2:
        return by_source(list(both[0]))
    me = lax.axis_index("dp")
    low = by_source(list(lax.dynamic_index_in_dim(both, me, 0, keepdims=False)))
    high = by_source(list(lax.dynamic_index_in_dim(both, 1 - me, 0, keepdims=False)))
    return [jnp.concatenate(pair, axis=0) for pair in zip(low, high)]


def pair_halves(grad):
    count = lax.axis_size("row")
    rows = grad.shape[0] // count
    if lax.axis_size("dp") != 2:
        total = grad.reshape(count, rows, grad.shape[1])
        return jnp.zeros_like(total), total
    me = lax.axis_index("dp")
    halves = row_major(grad.reshape(count, 2, rows // 2, grad.shape[1]))
    given = lax.dynamic_index_in_dim(halves, 1 - me, 1, keepdims=False)
    kept = lax.dynamic_index_in_dim(halves, me, 1, keepdims=False)
    return row_major(kept), row_major(given)


def pair_swap(given):
    return swap_dp(given) if lax.axis_size("dp") == 2 else lax.psum(given, "dp")


def dp_stack(values):
    if lax.axis_size("dp") == 2:
        both = jnp.stack([values, swap_dp(values)])
        me = lax.axis_index("dp")
        return jnp.stack(
            [
                lax.dynamic_index_in_dim(both, me, 0, keepdims=False),
                lax.dynamic_index_in_dim(both, 1 - me, 0, keepdims=False),
            ]
        )
    return lax.all_gather(values, "dp", axis=0, tiled=False)


def normalize(values):
    center = jnp.mean(values, axis=1, keepdims=True)
    centred = values - center
    spread_of = jnp.mean(centred * centred, axis=1, keepdims=True)
    inverse = lax.rsqrt(spread_of + norm_epsilon)
    return (centred * inverse, inverse)


def normalize_back(grad_values, normed, inverse):
    totals = jnp.mean(grad_values, axis=1, keepdims=True)
    along = jnp.mean(grad_values * normed, axis=1, keepdims=True)
    return inverse * (grad_values - totals - normed * along)


def shards(
    block_in,
    labels,
    steps_t,
    out_cot,
    class_table,
    w_ada,
    b_ada,
    w_qkv,
    b_qv,
    w_out,
    b_out,
    w_up,
    b_up,
    w_down,
    b_down,
):
    rows = lax.axis_size("row")
    me_row = lax.axis_index("row")
    me_col = lax.axis_index("col")
    tok_local, width_row = block_in.shape
    width = width_row * rows
    width_col = w_out.shape[0]
    heads_col = width_col // HD
    heads_own = max(1, heads_col // rows)
    copies = max(1, rows // heads_col)
    head_width = heads_own * HD
    head_groups = rows // copies
    units_own = w_up.shape[1] // rows

    tokens_mesh, mesh_tokens = block_places()
    tokens = tok_local * lax.axis_size("col")

    feature = me_col * width_col + jnp.arange(width_col)
    half_width = width // 2
    frequency = jnp.exp(
        -math.log(10000.0) * (feature % half_width).astype(jnp.float32) / half_width
    )
    angles = steps_t.astype(jnp.float32)[:, None] * frequency[None, :]
    own_class = lax.dynamic_slice_in_dim(class_table, labels[0], 1, 0)
    condition = own_class + jnp.where(
        feature[None, :] < half_width, jnp.cos(angles), jnp.sin(angles)
    )
    silu_cond, silu_pull = jax.vjp(jax.nn.silu, condition)
    both_own = row_parts(
        jnp.concatenate([block_in, out_cot], axis=1).reshape(
            rows, tok_local // rows, 2 * width_row
        )
    )
    both_own = by_source(both_own)
    in_own = jnp.concatenate([part[:, :width_row] for part in both_own], axis=1)
    cot_own = jnp.concatenate([part[:, width_row:] for part in both_own], axis=1)
    silu_now, qkv_now, out_now, up_now, down_now = after(
        (silu_cond, w_qkv, w_out, w_up, w_down), in_own
    )
    ada_terms = jnp.sum(silu_now[0][:, None, None] * w_ada, axis=0)

    qkv_blocks = (
        qkv_now.reshape(width_row, 3, head_groups, head_width)
        .transpose(2, 0, 1, 3)
        .reshape(head_groups, width_row, 3 * head_width)
    )
    out_blocks = out_now.reshape(head_groups, head_width, width_row).transpose(0, 2, 1)
    head_blocks = jnp.concatenate([qkv_blocks, out_blocks], axis=2)
    head_blocks = own_half(jnp.repeat(head_blocks, copies, axis=0), 1)
    mlp_blocks = own_half(
        jnp.stack(
            [
                jnp.concatenate(
                    [
                        up_now[:, i * units_own : (i + 1) * units_own],
                        down_now[i * units_own : (i + 1) * units_own].T,
                    ],
                    axis=1,
                )
                for i in range(rows)
            ]
        ),
        1,
    )
    mlp_sent = row_outgoing(mlp_blocks)
    in_pieces, mlp_sent = spread(in_own, mlp_sent)
    ada_terms = butterfly(ada_terms, "col") + b_ada
    head_blocks = move_rows(head_blocks)
    mlp_blocks = row_major(jnp.stack(row_send(mlp_sent)))
    small = jnp.concatenate([ada_terms, b_out[None], b_down[None]], axis=0)
    small = [shift_row(small, step) for step in range(rows)]
    small = by_source(after(small, in_pieces[1]))
    small = jnp.concatenate(small, axis=1)[:, None, :]
    shift_one, scale_one, gate_one, shift_two, scale_two, gate_two, out_bias, down_bias = small

    head_blocks = share_blocks(head_blocks)
    head_matrix = jnp.concatenate(order_blocks(after(head_blocks, in_pieces[1])), axis=0)
    qkv_matrix = head_matrix[:, : 3 * head_width]
    out_flip = head_matrix[:, 3 * head_width :]
    normed_one, inverse_one = normalize(in_own)
    hidden_one = [normalize(piece)[0] * (1.0 + scale_one) + shift_one for piece in in_pieces]
    head_start = (me_row // copies) * head_width
    head_bias = lax.dynamic_slice_in_dim(b_qv, head_start, head_width, 1)
    qkv = by_piece(lambda piece: contract(piece, qkv_matrix, 1, 0), hidden_one)
    qkv = qkv.reshape(tokens, 3, heads_own, HD)
    queries = qkv[:, 0] + head_bias[0].reshape(heads_own, HD)
    keys = qkv[:, 1]
    values = qkv[:, 2] + head_bias[1].reshape(heads_own, HD)
    factor = 1.0 / math.sqrt(HD)
    scores = jnp.einsum("qhd,khd->hqk", queries, keys, precision=fast_mode) * factor
    weights = jnp.exp(scores)
    weights = weights / jnp.sum(weights, axis=2, keepdims=True)
    attended = jnp.einsum("hqk,khd->qhd", weights, values, precision=fast_mode)
    attended = attended.reshape(tokens, head_width)

    def share_mlp(earlier):
        return share_blocks(after(mlp_blocks, earlier))

    attn_out, mlp_blocks = scatter_tokens(
        lambda start, size: contract(attended[start : start + size], out_flip, 1, 1)
        * (1.0 / copies),
        tokens,
        share_mlp,
    )
    attn_out = attn_out + out_bias
    mixed = in_own + gate_one * attn_out
    normed_two, inverse_two = normalize(mixed)
    hidden_two_own = normed_two * (1.0 + scale_two) + shift_two
    mlp_matrix = row_major(
        jnp.concatenate(order_blocks(after(mlp_blocks, hidden_two_own)), axis=0)
    )
    up_matrix = mlp_matrix[:, :units_own]
    down_matrix = mlp_matrix[:, units_own:]

    d_mlp_own = cot_own * gate_two
    cot_all = gather_mesh(after(cot_own, in_pieces[1]))
    d_activated = contract(cot_all, gate_two.reshape(width, 1) * down_matrix, 1, 0)
    d_activated = take_blocks(d_activated, tokens_mesh)
    hidden_two, (up_matrix, down_matrix, d_activated) = spread(
        hidden_two_own, (up_matrix, down_matrix, d_activated)
    )
    up_bias = lax.dynamic_slice_in_dim(b_up, me_row * units_own, units_own, 0)
    up_values = by_piece(lambda piece: contract(piece, up_matrix, 1, 0), hidden_two) + up_bias
    activated, gelu_pull = jax.vjp(partial(jax.nn.gelu, approximate=True), up_values)
    (d_up,) = gelu_pull(d_activated)

    def mlp_rest(earlier):
        activated_mesh = take_blocks(after(activated, earlier), mesh_tokens)
        up_grad = contract(jnp.concatenate(after(hidden_two, earlier)), d_up, 0, 0)
        down_grad = contract(cot_all, activated_mesh, 0, 0) * gate_two.reshape(width, 1)
        halves = pair_halves(jnp.concatenate([up_grad, down_grad], axis=1))
        return contract(activated_mesh, down_matrix, 1, 1), halves

    d_hidden_two, mlp_rest_done = scatter_tokens(
        lambda start, size: contract(d_up[start : start + size], up_matrix, 1, 1), tokens, mlp_rest
    )

    d_mixed = cot_own + normalize_back(d_hidden_two * (1.0 + scale_two), normed_two, inverse_two)
    d_attn_own = d_mixed * gate_one
    d_attn, (mlp_part, (mlp_kept, mlp_given)) = spread(d_attn_own, mlp_rest_done)
    mlp_own = scatter_mesh(mlp_part)
    mlp_given = pair_swap(mlp_given)
    d_attended = by_piece(lambda piece: contract(piece, out_flip, 1, 0), d_attn)
    d_attended = d_attended.reshape(tokens, heads_own, HD)
    d_weights = jnp.einsum("qhd,khd->hqk", d_attended, values, precision=fast_mode)
    row_dots = jnp.sum(weights * d_weights, axis=2, keepdims=True)
    d_scores = weights * (d_weights - row_dots) * factor
    d_query = jnp.einsum("hqk,khd->qhd", d_scores, keys, precision=fast_mode)
    d_key = jnp.einsum("hqk,qhd->khd", d_scores, queries, precision=fast_mode)
    d_value = jnp.einsum("hqk,qhd->khd", weights, d_attended, precision=fast_mode)
    d_qkv = jnp.stack([d_query, d_key, d_value], axis=1).reshape(tokens, 3 * head_width)

    mlp_kept, mlp_given = after((mlp_kept, mlp_given), d_qkv)
    mlp_sent = row_outgoing(row_major(mlp_kept + mlp_given))

    def head_rest(earlier):
        mlp_moved = row_major(jnp.stack(row_send(after(mlp_sent, earlier))))
        d_heads = after(d_qkv, earlier)
        qkv_grad = contract(jnp.concatenate(hidden_one), d_heads, 0, 0)
        out_grad = contract(jnp.concatenate(d_attn), after(attended, earlier), 0, 0)
        kept, given = pair_halves(jnp.concatenate([qkv_grad, out_grad], axis=1))
        given = pair_swap(given)
        return mlp_moved, kept, given

    def head_rest_row(earlier, filled):
        mlp_moved, kept, given = filled
        return share_blocks(after(mlp_moved, earlier)), kept, given

    d_hidden_one, (mlp_shared, head_kept, head_given) = scatter_tokens(
        lambda start, size: contract(d_qkv[start : start + size], qkv_matrix, 1, 1)
        * (1.0 / copies),
        tokens,
        head_rest,
        head_rest_row,
    )
    mlp_own = after(mlp_own, d_hidden_one) + down_bias
    in_grad = d_mixed + normalize_back(
        d_hidden_one * (1.0 + scale_one), normed_one, inverse_one
    )
    block_out = mixed + gate_two * mlp_own
    results = jnp.stack(
        [
            jnp.concatenate(
                [
                    block_out[:, i * width_row : (i + 1) * width_row],
                    in_grad[:, i * width_row : (i + 1) * width_row],
                ],
                axis=1,
            )
            for i in range(rows)
        ]
    )
    results = row_parts(results)

    unit_sums = jnp.concatenate([jnp.sum(d_up, axis=0), jnp.sum(d_qkv, axis=0)])
    unit_sums = jnp.stack(by_source([shift_row(unit_sums, step) for step in range(rows)]))
    own_sums = jnp.stack(
        [
            jnp.sum(d_hidden_one, axis=0),
            jnp.sum(d_hidden_one * normed_one, axis=0),
            jnp.sum(d_mixed * attn_out, axis=0),
            jnp.sum(d_hidden_two, axis=0),
            jnp.sum(d_hidden_two * normed_two, axis=0),
            jnp.sum(cot_own * mlp_own, axis=0),
            jnp.sum(d_attn_own, axis=0),
            jnp.sum(d_mlp_own, axis=0),
        ]
    )
    own_sums = butterfly(own_sums, "col")
    head_kept, head_given = after((head_kept, head_given), own_sums)
    head_moved = move_rows(head_kept + head_given)
    own_sums = butterfly(own_sums, "row")
    head_grad = order_blocks(share_blocks(after(head_moved, own_sums)))[::copies]
    qkv_grad = jnp.stack(
        [part[:, : 3 * head_width].reshape(width_row, 3, head_width) for part in head_grad],
        axis=2,
    ).reshape(width_row, 3, width_col)
    out_grad = jnp.concatenate([part[:, 3 * head_width :].T for part in head_grad], axis=0)
    mlp_grad = order_blocks(after(mlp_shared, own_sums))
    up_grad = jnp.concatenate([part[:, :units_own] for part in mlp_grad], axis=1)
    down_grad = jnp.concatenate([part[:, units_own:].T for part in mlp_grad], axis=0)
    own_sums = lax.dynamic_slice_in_dim(own_sums, me_row * width_row, width_row, 1)
    results = jnp.concatenate(by_source(after(results, own_sums)), axis=0)
    label_row = jnp.broadcast_to(labels.astype(jnp.float32), (128,))
    unit_size = unit_sums.size
    pack = dp_stack(
        jnp.concatenate([unit_sums.reshape(-1), own_sums.reshape(-1), silu_cond[0], label_row])
    )
    unit_sums = jnp.sum(pack[:, :unit_size], axis=0).reshape(rows, -1)
    up_bias_grad = unit_sums[:, :units_own].reshape(-1)
    qkv_sums = unit_sums[::copies, units_own:].reshape(head_groups, 3, head_width)
    qv_bias_grad = jnp.stack([qkv_sums[:, 0].reshape(-1), qkv_sums[:, 2].reshape(-1)])
    sums_all = pack[:, unit_size : unit_size + 8 * width_row].reshape(-1, 8, width_row)
    silu_all = pack[:, unit_size + 8 * width_row : -128]
    bias_sums = jnp.sum(sums_all, axis=0)
    ada_grad = jnp.sum(silu_all[:, :, None, None] * sums_all[:, None, :6], axis=0)
    silu_grads = jnp.sum(own_sums[None, :6] * w_ada, axis=(1, 2))[None]
    silu_grads = butterfly(silu_grads, "row")
    (cond_grad,) = silu_pull(silu_grads)
    cond_all = dp_stack(cond_grad[0])
    label_all = pack[:, -1].astype(jnp.int32)
    classes = jnp.arange(class_table.shape[0])
    table_grad = jnp.sum(
        jnp.where(
            label_all[:, None, None] == classes[None, :, None], cond_all[:, None, :], 0.0
        ),
        axis=0,
    )
    return (
        results[:, :width_row],
        results[:, width_row:],
        table_grad,
        ada_grad,
        bias_sums[:6],
        qkv_grad,
        qv_bias_grad,
        out_grad,
        bias_sums[6],
        up_grad,
        up_bias_grad,
        down_grad,
        bias_sums[7],
    )


def solution(mesh):
    in_specs = (
        P(("dp", "col"), "row"),
        P("dp"),
        P("dp"),
        P(("dp", "col"), "row"),
        P(None, "col"),
        P("col", None, "row"),
        P(None, "row"),
        P("row", None, "col"),
        P(None, "col"),
        P("col", "row"),
        P("row"),
        P("row", "col"),
        P("col"),
        P("col", "row"),
        P("row"),
    )
    out_specs = (
        P(("dp", "col"), "row"),
        P(("dp", "col"), "row"),
        P(None, "col"),
        P("col", None, "row"),
        P(None, "row"),
        P("row", None, "col"),
        P(None, "col"),
        P("col", "row"),
        P("row"),
        P("row", "col"),
        P("col"),
        P("col", "row"),
        P("row"),
    )

    return jax.shard_map(shards, mesh=mesh, in_specs=in_specs, out_specs=out_specs, check_vma=False)
```

profile of v0, /device:TPU:0, one launch (start us, length us, event | category | flops | bytes accessed | tf_op | source)
XLA Modules:
  0.0 671.2 jit_solution(6211533980867175055)
XLA Ops:
  9.9 5.1 collective-permute-start.2
  20.3 8.7 %collective-permute-done.1 = f32[64,576]{1,0:T(8,128)S(1)} collective-permute-done((f32[64,576]{1,0:T(8,128)S(1)}, f32[64,576]{1,0:T(8,128)S(1)}, u32[]{:S(2)}, u32[]{:S(2)}) %collective-permute-start.1) | collective-permute-done | bytes 147488 | tf_op jit(solution)/shard_map/ppermute | solution.py:36
  53.1 2.3 collective-permute-start.16
  57.5 9.5 %collective-permute-done.16 = f32[144,288]{1,0:T(8,128)S(1)} collective-permute-done((f32[144,288]{1,0:T(8,128)S(1)}, f32[144,288]{1,0:T(8,128)S(1)}, u32[]{:S(2)}, u32[]{:S(2)}) %collective-permute-start.16) | collective-permute-done | bytes 165920 | tf_op jit(solution)/shard_map/ppermute | solution.py:36
  67.0 5.9 collective-permute-start.7
  80.0 4.6 collective-permute-done.13
  86.5 5.0 collective-permute-done.14
  91.5 2.7 collective-permute-start.10
  94.4 5.9 collective-permute-done.10
  143.3 3.3 collective-permute-done.26
  148.3 8.4 %collective-permute-done.27 = f32[64,1152]{1,0:T(8,128)S(1)} collective-permute-done((f32[64,1152]{1,0:T(8,128)S(1)}, f32[64,1152]{1,0:T(8,128)S(1)}, u32[]{:S(2)}, u32[]{:S(2)}) %collective-permute-start.27) | collective-permute-done | bytes 294944 | tf_op jit(solution)/shard_map/ppermute | solution.py:46
  157.5 3.3 collective-permute-start.28
  168.6 4.3 collective-permute-start.34
  173.7 5.8 collective-permute-done.23
  180.8 3.8 collective-permute-start.29
  184.6 10.5 %collective-permute-done.33 = f32[144,576]{1,0:T(8,128)S(1)} collective-permute-done((f32[144,576]{1,0:T(8,128)}, f32[144,576]{1,0:T(8,128)S(1)}, u32[]{:S(2)}, u32[]{:S(2)}) %collective-permute-start.33) | collective-permute-done | bytes 331808 | tf_op jit(solution)/shard_map/ppermute | solution.py:36
  196.8 4.6 collective-permute-done.24
  201.4 3.7 collective-permute-done.29
  208.3 6.5 collective-permute-start.31
  216.8 9.3 %collective-permute-done.35 = f32[4,144,576]{2,1,0:T(8,128)S(1)} collective-permute-done((f32[4,144,576]{2,1,0:T(8,128)S(1)}, f32[4,144,576]{2,1,0:T(8,128)S(1)}, u32[]{:S(2)}, u32[]{:S(2)}) %collective-permute-start.35) | collective-permute-done | bytes 1327136 | tf_op jit(solution)/shard_map/ppermute | solution.py:54
  233.0 3.8 fusion.156
  236.8 8.3 %fusion.18.source_ref = f32[1024,288]{1,0:T(8,128)} fusion(f32[1024,1152]{1,0:T(8,128)} %all-gather.2.cloned.1.call-done, f32[1152]{0:T(1024)S(1)} %get-tuple-element.169, f32[1152,576]{1,0:T(8,128)} %bitcast_dynamic-update-slice_fusion), kind=kOutput, calls=%fused_computation.51 | convolution fusion | flops 2038763520 | bytes 7672320 | tf_op jit(solution)/shard_map/dot_general | solution.py:19
  245.0 2.8 take_blocks.2
  253.2 2.7 collective-permute-done.37
  259.8 17.8 %collective-permute-start.39 = (f32[64,1152]{1,0:T(8,128)}, f32[64,1152]{1,0:T(8,128)}, u32[]{:S(2)}, u32[]{:S(2)}) collective-permute-start(f32[64,1152]{1,0:T(8,128)} %collective-permute-done.30), channel_id=1, source_target_pairs={{0,4},{4,8},{8,12},{12,0},{1,5},{5,9},{9,13},{13,1},{2,6},{6,10},{... | collective-permute-start | bytes 884744 | tf_op jit(solution)/shard_map/ppermute | solution.py:36
  277.6 11.8 %collective-permute-done.39 = f32[64,1152]{1,0:T(8,128)} collective-permute-done((f32[64,1152]{1,0:T(8,128)}, f32[64,1152]{1,0:T(8,128)}, u32[]{:S(2)}, u32[]{:S(2)}) %collective-permute-start.39) | collective-permute-done | bytes 294944 | tf_op jit(solution)/shard_map/ppermute | solution.py:36
  291.7 6.8 %collective-permute-done.40 = f32[64,1152]{1,0:T(8,128)} collective-permute-done((f32[64,1152]{1,0:T(8,128)}, f32[64,1152]{1,0:T(8,128)}, u32[]{:S(2)}, u32[]{:S(2)}) %collective-permute-start.40) | collective-permute-done | bytes 294944 | tf_op jit(solution)/shard_map/ppermute | solution.py:46
  299.6 3.3 fusion.168
  304.5 3.3 fusion.170
  307.7 2.9 fusion.147
  314.0 2.9 collective-permute-done.48
  319.3 8.1 %collective-permute-done.49 = f32[64,1152]{1,0:T(8,128)S(1)} collective-permute-done((f32[64,1152]{1,0:T(8,128)S(1)}, f32[64,1152]{1,0:T(8,128)S(1)}, u32[]{:S(2)}, u32[]{:S(2)}) %collective-permute-start.49) | collective-permute-done | bytes 294944 | tf_op jit(solution)/shard_map/ppermute | solution.py:46
  336.0 3.2 take_blocks.3
  339.3 8.3 %fusion.172 = f32[1024,1152]{1,0:T(8,128)} fusion(f32[1024,288]{1,0:T(8,128)} %take_blocks.3, f32[1152,288]{1,0:T(8,128)} %get-tuple-element.89), kind=kOutput, calls=%fused_computation.500 | convolution fusion | flops 2038431744 | bytes 7225344 | tf_op jit(solution)/shard_map/dot_general | solution.py:19
  347.6 6.5 convolution_multiply_fusion
  354.2 5.7 fusion
  361.8 3.3 collective-permute-start.51
  365.7 7.2 %collective-permute-done.46 = f32[64,1152]{1,0:T(8,128)S(1)} collective-permute-done((f32[64,1152]{1,0:T(8,128)S(1)}, f32[64,1152]{1,0:T(8,128)S(1)}, u32[]{:S(2)}, u32[]{:S(2)}) %collective-permute-start.46) | collective-permute-done | bytes 294944 | tf_op jit(solution)/shard_map/ppermute | solution.py:36
  383.5 5.8 collective-permute-done.53
  389.3 3.7 collective-permute-done.52
  397.2 6.2 collective-permute-done.55
  408.9 8.0 %collective-permute-done.58 = f32[64,1152]{1,0:T(8,128)S(1)} collective-permute-done((f32[64,1152]{1,0:T(8,128)S(1)}, f32[64,1152]{1,0:T(8,128)S(1)}, u32[]{:S(2)}, u32[]{:S(2)}) %collective-permute-start.58) | collective-permute-done | bytes 294944 | tf_op jit(solution)/shard_map/ppermute | solution.py:46
  421.6 2.7 fusion.64
  429.7 2.6 multiply_reduce_fusion.1
  437.0 3.1 fusion.29
  443.9 2.5 collective-permute-start.79
  448.8 6.3 collective-permute-done.89
  457.8 3.0 fusion.36
  469.5 7.6 %collective-permute-done.67 = f32[64,1152]{1,0:T(8,128)S(1)} collective-permute-done((f32[64,1152]{1,0:T(8,128)S(1)}, f32[64,1152]{1,0:T(8,128)S(1)}, u32[]{:S(2)}, u32[]{:S(2)}) %collective-permute-start.67) | collective-permute-done | bytes 294944 | tf_op jit(solution)/shard_map/ppermute | solution.py:46
  477.9 2.7 collective-permute-start.68
  480.6 3.4 convolution_add_fusion
  484.1 2.3 collective-permute-start.91
  491.7 3.7 fusion.173
  498.6 3.4 collective-permute-done.68
  503.9 13.2 %collective-permute-start.69 = (f32[64,1152]{1,0:T(8,128)S(1)}, f32[64,1152]{1,0:T(8,128)S(1)}, u32[]{:S(2)}, u32[]{:S(2)}) collective-permute-start(f32[64,1152]{1,0:T(8,128)S(1)} %get-tuple-element.190), channel_id=1, source_target_pairs={{0,12},{4,0},{8,4},{12,8},{1,13},{5,1},{9,5},{13,9},{2,14},{6,2},{... | collective-permute-start | bytes 884744 | tf_op jit(solution)/shard_map/ppermute | solution.py:36
  517.4 5.6 collective-permute-done.91
  529.9 4.9 collective-permute-done.69
  537.8 23.9 %collective-permute-done.93 = f32[4,144,576]{2,1,0:T(8,128)S(1)} collective-permute-done((f32[4,144,576]{2,1,0:T(8,128)S(1)}, f32[4,144,576]{2,1,0:T(8,128)S(1)}, u32[]{:S(2)}, u32[]{:S(2)}) %collective-permute-start.93) | collective-permute-done | bytes 1327136 | tf_op jit(solution)/shard_map/ppermute | solution.py:54
  570.8 3.1 collective-permute-done.74
  573.8 12.5 %collective-permute-start.75 = (f32[8,1152]{1,0:T(8,128)S(1)}, f32[8,1152]{1,0:T(8,128)S(1)}, u32[]{:S(2)}, u32[]{:S(2)}) collective-permute-start(f32[8,1152]{1,0:T(8,128)S(1)} %add.871), channel_id=1, source_target_pairs={{0,4},{4,0},{8,12},{12,8},{1,5},{5,1},{9,13},{13,9},{2,6},{6,2},{1... | collective-permute-start | bytes 110600 | tf_op jit(solution)/shard_map/ppermute | solution.py:61
  595.7 15.0 %collective-permute-done.76 = f32[8,1152]{1,0:T(8,128)S(1)} collective-permute-done((f32[8,1152]{1,0:T(8,128)S(1)}, f32[8,1152]{1,0:T(8,128)S(1)}, u32[]{:S(2)}, u32[]{:S(2)}) %collective-permute-start.76) | collective-permute-done | bytes 36896 | tf_op jit(solution)/shard_map/ppermute | solution.py:61
  612.0 3.8 collective-permute-start.87
  628.0 3.7 collective-permute-done.82
  647.3 11.9 %collective-permute-done.88 = f32[4,144,288]{2,1,0:T(8,128)S(1)} collective-permute-done((f32[4,144,288]{2,1,0:T(8,128)S(1)}, f32[4,144,288]{2,1,0:T(8,128)S(1)}, u32[]{:S(2)}, u32[]{:S(2)}) %collective-permute-start.88) | collective-permute-done | bytes 663584 | tf_op jit(solution)/shard_map/ppermute | solution.py:54
  (626 shorter events, 267.1 us)
Async XLA Ops:
  7.2 229.6 %all-gather.2.cloned.1.call-start = ((), (), s32[]{:S(2)}) async-start(), calls=%async_computation.1 | async-start | bytes 5013504 | tf_op jit(solution)/shard_map/all_gather | solution.py:173
  15.1 13.9 %collective-permute-start.1 = (f32[64,576]{1,0:T(8,128)S(1)}, f32[64,576]{1,0:T(8,128)S(1)}, u32[]{:S(2)}, u32[]{:S(2)}) collective-permute-start(f32[64,576]{1,0:T(8,128)S(1)} %get-tuple-element.323), channel_id=1, source_target_pairs={{0,8},{4,12},{8,0},{12,4},{1,9},{5,13},{9,1},{13,5},{2,10},{6,14},... | collective-permute-start | bytes 442376 | tf_op jit(solution)/shard_map/ppermute | solution.py:36
  15.1 13.9 %collective-permute-start = (f32[64,576]{1,0:T(8,128)S(1)}, f32[64,576]{1,0:T(8,128)S(1)}, u32[]{:S(2)}, u32[]{:S(2)}) collective-permute-start(f32[64,576]{1,0:T(8,128)S(1)} %get-tuple-element.324), channel_id=1, source_target_pairs={{0,4},{4,8},{8,12},{12,0},{1,5},{5,9},{9,13},{13,1},{2,6},{6,10},{... | collective-permute-start | bytes 442376 | tf_op jit(solution)/shard_map/ppermute | solution.py:36
  32.1 45.1 %collective-permute-start.12 = (f32[64,1152]{1,0:T(8,128)S(1)}, f32[64,1152]{1,0:T(8,128)}, u32[]{:S(2)}, u32[]{:S(2)}) collective-permute-start(f32[64,1152]{1,0:T(8,128)S(1)} %concatenate.134), channel_id=1, source_target_pairs={{0,2},{1,3},{2,0},{3,1},{4,6},{5,7},{6,4},{7,5},{8,10},{9,11},{10,... | collective-permute-start | bytes 884744 | tf_op jit(solution)/shard_map/ppermute | solution.py:46
  33.6 41.5 %collective-permute-start.9 = (f32[64,1152]{1,0:T(8,128)S(1)}, f32[64,1152]{1,0:T(8,128)}, u32[]{:S(2)}, u32[]{:S(2)}) collective-permute-start(f32[64,1152]{1,0:T(8,128)S(1)} %concatenate.134), channel_id=1, source_target_pairs={{0,12},{4,0},{8,4},{12,8},{1,13},{5,1},{9,5},{13,9},{2,14},{6,2},{... | collective-permute-start | bytes 884744 | tf_op jit(solution)/shard_map/ppermute | solution.py:36
  34.7 41.0 %collective-permute-start.8 = (f32[64,1152]{1,0:T(8,128)S(1)}, f32[64,1152]{1,0:T(8,128)}, u32[]{:S(2)}, u32[]{:S(2)}) collective-permute-start(f32[64,1152]{1,0:T(8,128)S(1)} %concatenate.134), channel_id=1, source_target_pairs={{0,4},{4,8},{8,12},{12,0},{1,5},{5,9},{9,13},{13,1},{2,6},{6,10},{... | collective-permute-start | bytes 884744 | tf_op jit(solution)/shard_map/ppermute | solution.py:36
  53.1 13.9 %collective-permute-start.16 = (f32[144,288]{1,0:T(8,128)S(1)}, f32[144,288]{1,0:T(8,128)S(1)}, u32[]{:S(2)}, u32[]{:S(2)}) collective-permute-start(f32[144,288]{1,0:T(8,128)S(1)} %get-tuple-element.250), channel_id=1, source_target_pairs={{0,8},{4,12},{8,0},{12,4},{1,9},{5,13},{9,1},{13,5},{2,10},{6,14},... | collective-permute-start | bytes 497672 | tf_op jit(solution)/shard_map/ppermute | solution.py:36
  55.9 17.0 %collective-permute-start.17 = (f32[144,288]{1,0:T(8,128)S(1)}, f32[144,288]{1,0:T(8,128)S(1)}, u32[]{:S(2)}, u32[]{:S(2)}) collective-permute-start(f32[144,288]{1,0:T(8,128)S(1)} %get-tuple-element.251), channel_id=1, source_target_pairs={{0,12},{4,0},{8,4},{12,8},{1,13},{5,1},{9,5},{13,9},{2,14},{6,2},{... | collective-permute-start | bytes 497672 | tf_op jit(solution)/shard_map/ppermute | solution.py:36
  67.0 42.3 %collective-permute-start.7 = (f32[8,288]{1,0:T(8,128)S(1)}, f32[8,288]{1,0:T(8,128)}, u32[]{:S(2)}, u32[]{:S(2)}) collective-permute-start(f32[8,288]{1,0:T(8,128)S(1)} %pad_maximum_fusion.41), channel_id=1, source_target_pairs={{0,12},{4,0},{8,4},{12,8},{1,13},{5,1},{9,5},{13,9},{2,14},{6,2},{... | collective-permute-start | bytes 27656 | tf_op jit(solution)/shard_map/ppermute | solution.py:36
  72.9 36.4 %collective-permute-start.6 = (f32[8,288]{1,0:T(8,128)S(1)}, f32[8,288]{1,0:T(8,128)}, u32[]{:S(2)}, u32[]{:S(2)}) collective-permute-start(f32[8,288]{1,0:T(8,128)S(1)} %pad_maximum_fusion.41), channel_id=1, source_target_pairs={{0,8},{4,12},{8,0},{12,4},{1,9},{5,13},{9,1},{13,5},{2,10},{6,14},... | collective-permute-start | bytes 27656 | tf_op jit(solution)/shard_map/ppermute | solution.py:36
  75.1 34.2 %collective-permute-start.5 = (f32[8,288]{1,0:T(8,128)S(1)}, f32[8,288]{1,0:T(8,128)}, u32[]{:S(2)}, u32[]{:S(2)}) collective-permute-start(f32[8,288]{1,0:T(8,128)S(1)} %pad_maximum_fusion.41), channel_id=1, source_target_pairs={{0,4},{4,8},{8,12},{12,0},{1,5},{5,9},{9,13},{13,1},{2,6},{6,10},{... | collective-permute-start | bytes 27656 | tf_op jit(solution)/shard_map/ppermute | solution.py:36
  75.7 28.1 %collective-permute-start.18 = (f32[4,144,288]{2,1,0:T(8,128)}, f32[4,144,288]{2,1,0:T(8,128)S(1)}, u32[]{:S(2)}, u32[]{:S(2)}) collective-permute-start(f32[4,144,288]{2,1,0:T(8,128)} %get-tuple-element.300), channel_id=1, source_target_pairs={{0,16},{16,0},{1,17},{17,1},{2,18},{18,2},{3,19},{19,3},{4,20},{20... | collective-permute-start | bytes 1990664 | tf_op jit(solution)/shard_map/ppermute | solution.py:54
  103.8 22.8 %collective-permute-start.19 = (f32[384,1152]{1,0:T(8,128)S(1)}, f32[384,1152]{1,0:T(8,128)}, u32[]{:S(2)}, u32[]{:S(2)}) collective-permute-start(f32[384,1152]{1,0:T(8,128)S(1)} %constant_dynamic-update-slice_fusion.2), channel_id=1, source_target_pairs={{0,1},{1,0},{2,3},{3,2},{4,5},{5,4},{6,7},{7,6},{8,9},{9,8},{10,11... | collective-permute-start | bytes 5308424 | tf_op jit(solution)/shard_map/ppermute | solution.py:50
  110.7 451.2 %reduce-scatter.2.cloned.1.call-start = ((), (), s32[]{:S(2)}) async-start(), calls=%async_computation.2 | async-start | bytes 5013504 | tf_op jit(solution)/shard_map/reduce_scatter | solution.py:177
  141.8 19.0 %collective-permute-start.21 = (f32[384,1152]{1,0:T(8,128)S(1)}, f32[384,1152]{1,0:T(8,128)S(1)}, u32[]{:S(2)}, u32[]{:S(2)}) collective-permute-start(f32[384,1152]{1,0:T(8,128)S(1)} %fusion.69), channel_id=1, source_target_pairs={{0,1},{1,0},{2,3},{3,2},{4,5},{5,4},{6,7},{7,6},{8,9},{9,8},{10,11... | collective-permute-start | bytes 5308424 | tf_op jit(solution)/shard_map/ppermute | solution.py:50
  163.5 16.0 %collective-permute-start.23 = (f32[64,1152]{1,0:T(8,128)}, f32[64,1152]{1,0:T(8,128)}, u32[]{:S(2)}, u32[]{:S(2)}) collective-permute-start(f32[64,1152]{1,0:T(8,128)} %get-tuple-element.237), channel_id=1, source_target_pairs={{0,2},{1,3},{2,0},{3,1},{4,6},{5,7},{6,4},{7,5},{8,10},{9,11},{10,... | collective-permute-start | bytes 884744 | tf_op jit(solution)/shard_map/ppermute | solution.py:46
  165.6 15.1 %collective-permute-start.32 = (f32[144,576]{1,0:T(8,128)}, f32[144,576]{1,0:T(8,128)S(1)}, u32[]{:S(2)}, u32[]{:S(2)}) collective-permute-start(f32[144,576]{1,0:T(8,128)} %get-tuple-element.78), channel_id=1, source_target_pairs={{0,4},{4,8},{8,12},{12,0},{1,5},{5,9},{9,13},{13,1},{2,6},{6,10},{... | collective-permute-start | bytes 995336 | tf_op jit(solution)/shard_map/ppermute | solution.py:36
  165.7 29.4 %collective-permute-start.33 = (f32[144,576]{1,0:T(8,128)}, f32[144,576]{1,0:T(8,128)S(1)}, u32[]{:S(2)}, u32[]{:S(2)}) collective-permute-start(f32[144,576]{1,0:T(8,128)} %get-tuple-element.79), channel_id=1, source_target_pairs={{0,8},{4,12},{8,0},{12,4},{1,9},{5,13},{9,1},{13,5},{2,10},{6,14},... | collective-permute-start | bytes 995336 | tf_op jit(solution)/shard_map/ppermute | solution.py:36
  168.6 26.6 %collective-permute-start.34 = (f32[144,576]{1,0:T(8,128)}, f32[144,576]{1,0:T(8,128)S(1)}, u32[]{:S(2)}, u32[]{:S(2)}) collective-permute-start(f32[144,576]{1,0:T(8,128)} %get-tuple-element.80), channel_id=1, source_target_pairs={{0,12},{4,0},{8,4},{12,8},{1,13},{5,1},{9,5},{13,9},{2,14},{6,2},{... | collective-permute-start | bytes 995336 | tf_op jit(solution)/shard_map/ppermute | solution.py:36
  173.2 23.6 %collective-permute-start.22 = (f32[64,1152]{1,0:T(8,128)}, f32[64,1152]{1,0:T(8,128)S(1)}, u32[]{:S(2)}, u32[]{:S(2)}) collective-permute-start(f32[64,1152]{1,0:T(8,128)} %get-tuple-element.235), channel_id=1, source_target_pairs={{0,2},{1,3},{2,0},{3,1},{4,6},{5,7},{6,4},{7,5},{8,10},{9,11},{10,... | collective-permute-start | bytes 884744 | tf_op jit(solution)/shard_map/ppermute | solution.py:46
  180.7 20.7 %collective-permute-start.24 = (f32[64,1152]{1,0:T(8,128)S(1)}, f32[64,1152]{1,0:T(8,128)S(1)}, u32[]{:S(2)}, u32[]{:S(2)}) collective-permute-start(f32[64,1152]{1,0:T(8,128)S(1)} %get-tuple-element.238), channel_id=1, source_target_pairs={{0,4},{4,8},{8,12},{12,0},{1,5},{5,9},{9,13},{13,1},{2,6},{6,10},{... | collective-permute-start | bytes 884744 | tf_op jit(solution)/shard_map/ppermute | solution.py:36
  180.8 24.2 %collective-permute-start.29 = (f32[64,1152]{1,0:T(8,128)S(1)}, f32[64,1152]{1,0:T(8,128)S(1)}, u32[]{:S(2)}, u32[]{:S(2)}) collective-permute-start(f32[64,1152]{1,0:T(8,128)S(1)} %get-tuple-element.239), channel_id=1, source_target_pairs={{0,12},{4,0},{8,4},{12,8},{1,13},{5,1},{9,5},{13,9},{2,14},{6,2},{... | collective-permute-start | bytes 884744 | tf_op jit(solution)/shard_map/ppermute | solution.py:36
  195.2 30.8 %collective-permute-start.35 = (f32[4,144,576]{2,1,0:T(8,128)S(1)}, f32[4,144,576]{2,1,0:T(8,128)S(1)}, u32[]{:S(2)}, u32[]{:S(2)}) collective-permute-start(f32[4,144,576]{2,1,0:T(8,128)S(1)} %pad_maximum_fusion.5), channel_id=1, source_target_pairs={{0,16},{16,0},{1,17},{17,1},{2,18},{18,2},{3,19},{19,3},{4,20},{20... | collective-permute-start | bytes 3981320 | tf_op jit(solution)/shard_map/ppermute | solution.py:54
  207.7 40.7 %collective-permute-start.36 = (f32[64,1152]{1,0:T(8,128)}, f32[64,1152]{1,0:T(8,128)}, u32[]{:S(2)}, u32[]{:S(2)}) collective-permute-start(f32[64,1152]{1,0:T(8,128)} %get-tuple-element.194), channel_id=1, source_target_pairs={{0,2},{1,3},{2,0},{3,1},{4,6},{5,7},{6,4},{7,5},{8,10},{9,11},{10,... | collective-permute-start | bytes 884744 | tf_op jit(solution)/shard_map/ppermute | solution.py:46
  208.3 39.5 %collective-permute-start.31 = (f32[64,1152]{1,0:T(8,128)}, f32[64,1152]{1,0:T(8,128)}, u32[]{:S(2)}, u32[]{:S(2)}) collective-permute-start(f32[64,1152]{1,0:T(8,128)} %get-tuple-element.194), channel_id=1, source_target_pairs={{0,12},{4,0},{8,4},{12,8},{1,13},{5,1},{9,5},{13,9},{2,14},{6,2},{... | collective-permute-start | bytes 884744 | tf_op jit(solution)/shard_map/ppermute | solution.py:36
  214.8 33.0 %collective-permute-start.30 = (f32[64,1152]{1,0:T(8,128)}, f32[64,1152]{1,0:T(8,128)}, u32[]{:S(2)}, u32[]{:S(2)}) collective-permute-start(f32[64,1152]{1,0:T(8,128)} %get-tuple-element.194), channel_id=1, source_target_pairs={{0,4},{4,8},{8,12},{12,0},{1,5},{5,9},{9,13},{13,1},{2,6},{6,10},{... | collective-permute-start | bytes 884744 | tf_op jit(solution)/shard_map/ppermute | solution.py:36
  259.8 44.7 %collective-permute-start.41 = (f32[384,1152]{1,0:T(8,128)}, f32[384,1152]{1,0:T(8,128)}, u32[]{:S(2)}, u32[]{:S(2)}) collective-permute-start(f32[384,1152]{1,0:T(8,128)} %constant_dynamic-update-slice_fusion.8), channel_id=1, source_target_pairs={{0,1},{1,0},{2,3},{3,2},{4,5},{5,4},{6,7},{7,6},{8,9},{9,8},{10,11... | collective-permute-start | bytes 5308424 | tf_op jit(solution)/shard_map/ppermute | solution.py:50
  259.8 29.5 %collective-permute-start.39 = (f32[64,1152]{1,0:T(8,128)}, f32[64,1152]{1,0:T(8,128)}, u32[]{:S(2)}, u32[]{:S(2)}) collective-permute-start(f32[64,1152]{1,0:T(8,128)} %collective-permute-done.30), channel_id=1, source_target_pairs={{0,4},{4,8},{8,12},{12,0},{1,5},{5,9},{9,13},{13,1},{2,6},{6,10},{... | collective-permute-start | bytes 884744 | tf_op jit(solution)/shard_map/ppermute | solution.py:36
  312.4 17.2 %collective-permute-start.43 = (f32[384,1152]{1,0:T(8,128)S(1)}, f32[384,1152]{1,0:T(8,128)S(1)}, u32[]{:S(2)}, u32[]{:S(2)}) collective-permute-start(f32[384,1152]{1,0:T(8,128)S(1)} %fusion.47), channel_id=1, source_target_pairs={{0,1},{1,0},{2,3},{3,2},{4,5},{5,4},{6,7},{7,6},{8,9},{9,8},{10,11... | collective-permute-start | bytes 5308424 | tf_op jit(solution)/shard_map/ppermute | solution.py:50
  328.1 31.8 %collective-permute-start.50 = (f32[64,1152]{1,0:T(8,128)}, f32[64,1152]{1,0:T(8,128)}, u32[]{:S(2)}, u32[]{:S(2)}) collective-permute-start(f32[64,1152]{1,0:T(8,128)} %slice_add_fusion.4), channel_id=1, source_target_pairs={{0,12},{4,0},{8,4},{12,8},{1,13},{5,1},{9,5},{13,9},{2,14},{6,2},{... | collective-permute-start | bytes 884744 | tf_op jit(solution)/shard_map/ppermute | solution.py:36
  333.4 32.2 %collective-permute-start.44 = (f32[64,1152]{1,0:T(8,128)}, f32[64,1152]{1,0:T(8,128)}, u32[]{:S(2)}, u32[]{:S(2)}) collective-permute-start(f32[64,1152]{1,0:T(8,128)} %get-tuple-element.230), channel_id=1, source_target_pairs={{0,2},{1,3},{2,0},{3,1},{4,6},{5,7},{6,4},{7,5},{8,10},{9,11},{10,... | collective-permute-start | bytes 884744 | tf_op jit(solution)/shard_map/ppermute | solution.py:46
  334.0 25.9 %collective-permute-start.47 = (f32[64,1152]{1,0:T(8,128)}, f32[64,1152]{1,0:T(8,128)}, u32[]{:S(2)}, u32[]{:S(2)}) collective-permute-start(f32[64,1152]{1,0:T(8,128)} %get-tuple-element.231), channel_id=1, source_target_pairs={{0,2},{1,3},{2,0},{3,1},{4,6},{5,7},{6,4},{7,5},{8,10},{9,11},{10,... | collective-permute-start | bytes 884744 | tf_op jit(solution)/shard_map/ppermute | solution.py:46
  335.5 24.4 %collective-permute-start.45 = (f32[64,1152]{1,0:T(8,128)}, f32[64,1152]{1,0:T(8,128)}, u32[]{:S(2)}, u32[]{:S(2)}) collective-permute-start(f32[64,1152]{1,0:T(8,128)} %get-tuple-element.232), channel_id=1, source_target_pairs={{0,2},{1,3},{2,0},{3,1},{4,6},{5,7},{6,4},{7,5},{8,10},{9,11},{10,... | collective-permute-start | bytes 884744 | tf_op jit(solution)/shard_map/ppermute | solution.py:46
  361.8 13.4 %collective-permute-start.51 = (f32[64,1152]{1,0:T(8,128)S(1)}, f32[64,1152]{1,0:T(8,128)S(1)}, u32[]{:S(2)}, u32[]{:S(2)}) collective-permute-start(f32[64,1152]{1,0:T(8,128)S(1)} %get-tuple-element.234), channel_id=1, source_target_pairs={{0,12},{4,0},{8,4},{12,8},{1,13},{5,1},{9,5},{13,9},{2,14},{6,2},{... | collective-permute-start | bytes 884744 | tf_op jit(solution)/shard_map/ppermute | solution.py:36
  377.5 18.0 %collective-permute-start.54 = (f32[64,1152]{1,0:T(8,128)S(1)}, f32[64,1152]{1,0:T(8,128)S(1)}, u32[]{:S(2)}, u32[]{:S(2)}) collective-permute-start(f32[64,1152]{1,0:T(8,128)S(1)} %get-tuple-element.177), channel_id=1, source_target_pairs={{0,2},{1,3},{2,0},{3,1},{4,6},{5,7},{6,4},{7,5},{8,10},{9,11},{10,... | collective-permute-start | bytes 884744 | tf_op jit(solution)/shard_map/ppermute | solution.py:46
  393.0 14.4 %collective-permute-start.57 = (f32[64,1152]{1,0:T(8,128)S(1)}, f32[64,1152]{1,0:T(8,128)S(1)}, u32[]{:S(2)}, u32[]{:S(2)}) collective-permute-start(f32[64,1152]{1,0:T(8,128)S(1)} %collective-permute-done.52), channel_id=1, source_target_pairs={{0,4},{4,8},{8,12},{12,0},{1,5},{5,9},{9,13},{13,1},{2,6},{6,10},{... | collective-permute-start | bytes 884744 | tf_op jit(solution)/shard_map/ppermute | solution.py:36
  394.0 12.5 %collective-permute-start.56 = (f32[64,1152]{1,0:T(8,128)S(1)}, f32[64,1152]{1,0:T(8,128)S(1)}, u32[]{:S(2)}, u32[]{:S(2)}) collective-permute-start(f32[64,1152]{1,0:T(8,128)S(1)} %collective-permute-done.53), channel_id=1, source_target_pairs={{0,2},{1,3},{2,0},{3,1},{4,6},{5,7},{6,4},{7,5},{8,10},{9,11},{10,... | collective-permute-start | bytes 884744 | tf_op jit(solution)/shard_map/ppermute | solution.py:46
  407.4 21.1 %collective-permute-start.59 = (f32[384,1152]{1,0:T(8,128)}, f32[384,1152]{1,0:T(8,128)S(1)}, u32[]{:S(2)}, u32[]{:S(2)}) collective-permute-start(f32[384,1152]{1,0:T(8,128)} %get-tuple-element.333), channel_id=1, source_target_pairs={{0,1},{1,0},{2,3},{3,2},{4,5},{5,4},{6,7},{7,6},{8,9},{9,8},{10,11... | collective-permute-start | bytes 5308424 | tf_op jit(solution)/shard_map/ppermute | solution.py:50
  420.1 35.1 %collective-permute-start.89 = (f32[4,144,576]{2,1,0:T(8,128)}, f32[4,144,576]{2,1,0:T(8,128)}, u32[]{:S(2)}, u32[]{:S(2)}) collective-permute-start(f32[4,144,576]{2,1,0:T(8,128)} %get-tuple-element.108), channel_id=1, source_target_pairs={{0,16},{16,0},{1,17},{17,1},{2,18},{18,2},{3,19},{19,3},{4,20},{20... | collective-permute-start | bytes 3981320 | tf_op jit(solution)/shard_map/ppermute | solution.py:54
  443.9 24.9 %collective-permute-start.79 = (f32[504]{0:T(512)S(1)}, f32[504]{0:T(512)S(1)}, u32[]{:S(2)}, u32[]{:S(2)}) collective-permute-start(f32[504]{0:T(512)S(1)} %pad_maximum_fusion.47), channel_id=1, source_target_pairs={{0,12},{4,0},{8,4},{12,8},{1,13},{5,1},{9,5},{13,9},{2,14},{6,2},{... | collective-permute-start | bytes 6056 | tf_op jit(solution)/shard_map/ppermute | solution.py:36
  446.4 22.4 %collective-permute-start.78 = (f32[504]{0:T(512)S(1)}, f32[504]{0:T(512)S(1)}, u32[]{:S(2)}, u32[]{:S(2)}) collective-permute-start(f32[504]{0:T(512)S(1)} %pad_maximum_fusion.47), channel_id=1, source_target_pairs={{0,8},{4,12},{8,0},{12,4},{1,9},{5,13},{9,1},{13,5},{2,10},{6,14},... | collective-permute-start | bytes 6056 | tf_op jit(solution)/shard_map/ppermute | solution.py:36
  447.7 21.0 %collective-permute-start.77 = (f32[504]{0:T(512)S(1)}, f32[504]{0:T(512)S(1)}, u32[]{:S(2)}, u32[]{:S(2)}) collective-permute-start(f32[504]{0:T(512)S(1)} %pad_maximum_fusion.47), channel_id=1, source_target_pairs={{0,4},{4,8},{8,12},{12,0},{1,5},{5,9},{9,13},{13,1},{2,6},{6,10},{... | collective-permute-start | bytes 6056 | tf_op jit(solution)/shard_map/ppermute | solution.py:36
  460.7 19.8 %collective-permute-start.61 = (f32[384,1152]{1,0:T(8,128)}, f32[384,1152]{1,0:T(8,128)}, u32[]{:S(2)}, u32[]{:S(2)}) collective-permute-start(f32[384,1152]{1,0:T(8,128)} %fusion.36), channel_id=1, source_target_pairs={{0,1},{1,0},{2,3},{3,2},{4,5},{5,4},{6,7},{7,6},{8,9},{9,8},{10,11... | collective-permute-start | bytes 5308424 | tf_op jit(solution)/shard_map/ppermute | solution.py:50
  477.9 24.0 %collective-permute-start.68 = (f32[64,1152]{1,0:T(8,128)}, f32[64,1152]{1,0:T(8,128)}, u32[]{:S(2)}, u32[]{:S(2)}) collective-permute-start(f32[64,1152]{1,0:T(8,128)} %slice_add_fusion), channel_id=1, source_target_pairs={{0,12},{4,0},{8,4},{12,8},{1,13},{5,1},{9,5},{13,9},{2,14},{6,2},{... | collective-permute-start | bytes 884744 | tf_op jit(solution)/shard_map/ppermute | solution.py:36
  484.0 33.1 %collective-permute-start.90 = (f32[144,576]{1,0:T(8,128)}, f32[144,576]{1,0:T(8,128)}, u32[]{:S(2)}, u32[]{:S(2)}) collective-permute-start(f32[144,576]{1,0:T(8,128)} %get-tuple-element.112), channel_id=1, source_target_pairs={{0,4},{4,8},{8,12},{12,0},{1,5},{5,9},{9,13},{13,1},{2,6},{6,10},{... | collective-permute-start | bytes 995336 | tf_op jit(solution)/shard_map/ppermute | solution.py:36
  484.1 39.0 %collective-permute-start.91 = (f32[144,576]{1,0:T(8,128)}, f32[144,576]{1,0:T(8,128)}, u32[]{:S(2)}, u32[]{:S(2)}) collective-permute-start(f32[144,576]{1,0:T(8,128)} %get-tuple-element.113), channel_id=1, source_target_pairs={{0,8},{4,12},{8,0},{12,4},{1,9},{5,13},{9,1},{13,5},{2,10},{6,14},... | collective-permute-start | bytes 995336 | tf_op jit(solution)/shard_map/ppermute | solution.py:36
  487.4 14.5 %collective-permute-start.65 = (f32[64,1152]{1,0:T(8,128)}, f32[64,1152]{1,0:T(8,128)}, u32[]{:S(2)}, u32[]{:S(2)}) collective-permute-start(f32[64,1152]{1,0:T(8,128)} %get-tuple-element.227), channel_id=1, source_target_pairs={{0,2},{1,3},{2,0},{3,1},{4,6},{5,7},{6,4},{7,5},{8,10},{9,11},{10,... | collective-permute-start | bytes 884744 | tf_op jit(solution)/shard_map/ppermute | solution.py:46
  488.0 14.7 %collective-permute-start.63 = (f32[64,1152]{1,0:T(8,128)}, f32[64,1152]{1,0:T(8,128)}, u32[]{:S(2)}, u32[]{:S(2)}) collective-permute-start(f32[64,1152]{1,0:T(8,128)} %get-tuple-element.228), channel_id=1, source_target_pairs={{0,2},{1,3},{2,0},{3,1},{4,6},{5,7},{6,4},{7,5},{8,10},{9,11},{10,... | collective-permute-start | bytes 884744 | tf_op jit(solution)/shard_map/ppermute | solution.py:46
  501.9 23.3 %collective-permute-start.92 = (f32[144,576]{1,0:T(8,128)}, f32[144,576]{1,0:T(8,128)S(1)}, u32[]{:S(2)}, u32[]{:S(2)}) collective-permute-start(f32[144,576]{1,0:T(8,128)} %get-tuple-element.114), channel_id=1, source_target_pairs={{0,12},{4,0},{8,4},{12,8},{1,13},{5,1},{9,5},{13,9},{2,14},{6,2},{... | collective-permute-start | bytes 995336 | tf_op jit(solution)/shard_map/ppermute | solution.py:36
  501.9 27.9 %collective-permute-start.62 = (f32[64,1152]{1,0:T(8,128)}, f32[64,1152]{1,0:T(8,128)S(1)}, u32[]{:S(2)}, u32[]{:S(2)}) collective-permute-start(f32[64,1152]{1,0:T(8,128)} %get-tuple-element.226), channel_id=1, source_target_pairs={{0,2},{1,3},{2,0},{3,1},{4,6},{5,7},{6,4},{7,5},{8,10},{9,11},{10,... | collective-permute-start | bytes 884744 | tf_op jit(solution)/shard_map/ppermute | solution.py:46
  503.9 30.8 %collective-permute-start.69 = (f32[64,1152]{1,0:T(8,128)S(1)}, f32[64,1152]{1,0:T(8,128)S(1)}, u32[]{:S(2)}, u32[]{:S(2)}) collective-permute-start(f32[64,1152]{1,0:T(8,128)S(1)} %get-tuple-element.190), channel_id=1, source_target_pairs={{0,12},{4,0},{8,4},{12,8},{1,13},{5,1},{9,5},{13,9},{2,14},{6,2},{... | collective-permute-start | bytes 884744 | tf_op jit(solution)/shard_map/ppermute | solution.py:36
  517.1 17.6 %collective-permute-start.64 = (f32[64,1152]{1,0:T(8,128)S(1)}, f32[64,1152]{1,0:T(8,128)S(1)}, u32[]{:S(2)}, u32[]{:S(2)}) collective-permute-start(f32[64,1152]{1,0:T(8,128)S(1)} %get-tuple-element.229), channel_id=1, source_target_pairs={{0,4},{4,8},{8,12},{12,0},{1,5},{5,9},{9,13},{13,1},{2,6},{6,10},{... | collective-permute-start | bytes 884744 | tf_op jit(solution)/shard_map/ppermute | solution.py:36
  526.4 35.2 %collective-permute-start.93 = (f32[4,144,576]{2,1,0:T(8,128)S(1)}, f32[4,144,576]{2,1,0:T(8,128)S(1)}, u32[]{:S(2)}, u32[]{:S(2)}) collective-permute-start(f32[4,144,576]{2,1,0:T(8,128)S(1)} %pad_maximum_fusion.8), channel_id=1, source_target_pairs={{0,16},{16,0},{1,17},{17,1},{2,18},{18,2},{3,19},{19,3},{4,20},{20... | collective-permute-start | bytes 3981320 | tf_op jit(solution)/shard_map/ppermute | solution.py:54
  529.3 61.1 %collective-permute-start.84 = (f32[4,144,288]{2,1,0:T(8,128)}, f32[4,144,288]{2,1,0:T(8,128)}, u32[]{:S(2)}, u32[]{:S(2)}) collective-permute-start(f32[4,144,288]{2,1,0:T(8,128)} %get-tuple-element.224), channel_id=1, source_target_pairs={{0,16},{16,0},{1,17},{17,1},{2,18},{18,2},{3,19},{19,3},{4,20},{20... | collective-permute-start | bytes 1990664 | tf_op jit(solution)/shard_map/ppermute | solution.py:54
  573.8 17.9 %collective-permute-start.75 = (f32[8,1152]{1,0:T(8,128)S(1)}, f32[8,1152]{1,0:T(8,128)S(1)}, u32[]{:S(2)}, u32[]{:S(2)}) collective-permute-start(f32[8,1152]{1,0:T(8,128)S(1)} %add.871), channel_id=1, source_target_pairs={{0,4},{4,0},{8,12},{12,8},{1,5},{5,1},{9,13},{13,9},{2,6},{6,2},{1... | collective-permute-start | bytes 110600 | tf_op jit(solution)/shard_map/ppermute | solution.py:61
  587.2 24.9 %collective-permute-start.72 = (f32[64,576]{1,0:T(8,128)}, f32[64,576]{1,0:T(8,128)S(1)}, u32[]{:S(2)}, u32[]{:S(2)}) collective-permute-start(f32[64,576]{1,0:T(8,128)} %get-tuple-element.313), channel_id=1, source_target_pairs={{0,12},{4,0},{8,4},{12,8},{1,13},{5,1},{9,5},{13,9},{2,14},{6,2},{... | collective-permute-start | bytes 442376 | tf_op jit(solution)/shard_map/ppermute | solution.py:36
  587.8 28.0 %collective-permute-start.71 = (f32[64,576]{1,0:T(8,128)}, f32[64,576]{1,0:T(8,128)S(1)}, u32[]{:S(2)}, u32[]{:S(2)}) collective-permute-start(f32[64,576]{1,0:T(8,128)} %get-tuple-element.314), channel_id=1, source_target_pairs={{0,8},{4,12},{8,0},{12,4},{1,9},{5,13},{9,1},{13,5},{2,10},{6,14},... | collective-permute-start | bytes 442376 | tf_op jit(solution)/shard_map/ppermute | solution.py:36
  588.6 27.2 %collective-permute-start.70 = (f32[64,576]{1,0:T(8,128)}, f32[64,576]{1,0:T(8,128)}, u32[]{:S(2)}, u32[]{:S(2)}) collective-permute-start(f32[64,576]{1,0:T(8,128)} %get-tuple-element.315), channel_id=1, source_target_pairs={{0,4},{4,8},{8,12},{12,0},{1,5},{5,9},{9,13},{13,1},{2,6},{6,10},{... | collective-permute-start | bytes 442376 | tf_op jit(solution)/shard_map/ppermute | solution.py:36
  591.8 18.9 %collective-permute-start.76 = (f32[8,1152]{1,0:T(8,128)S(1)}, f32[8,1152]{1,0:T(8,128)S(1)}, u32[]{:S(2)}, u32[]{:S(2)}) collective-permute-start(f32[8,1152]{1,0:T(8,128)S(1)} %add.872), channel_id=1, source_target_pairs={{0,8},{4,12},{8,0},{12,4},{1,9},{5,13},{9,1},{13,5},{2,10},{6,14},... | collective-permute-start | bytes 110600 | tf_op jit(solution)/shard_map/ppermute | solution.py:61
  594.5 45.6 %collective-permute-start.86 = (f32[144,288]{1,0:T(8,128)}, f32[144,288]{1,0:T(8,128)}, u32[]{:S(2)}, u32[]{:S(2)}) collective-permute-start(f32[144,288]{1,0:T(8,128)} %get-tuple-element.290), channel_id=1, source_target_pairs={{0,8},{4,12},{8,0},{12,4},{1,9},{5,13},{9,1},{13,5},{2,10},{6,14},... | collective-permute-start | bytes 497672 | tf_op jit(solution)/shard_map/ppermute | solution.py:36
  610.7 29.4 %collective-permute-start.85 = (f32[144,288]{1,0:T(8,128)}, f32[144,288]{1,0:T(8,128)}, u32[]{:S(2)}, u32[]{:S(2)}) collective-permute-start(f32[144,288]{1,0:T(8,128)} %get-tuple-element.291), channel_id=1, source_target_pairs={{0,4},{4,8},{8,12},{12,0},{1,5},{5,9},{9,13},{13,1},{2,6},{6,10},{... | collective-permute-start | bytes 497672 | tf_op jit(solution)/shard_map/ppermute | solution.py:36
  612.0 28.2 %collective-permute-start.87 = (f32[144,288]{1,0:T(8,128)}, f32[144,288]{1,0:T(8,128)}, u32[]{:S(2)}, u32[]{:S(2)}) collective-permute-start(f32[144,288]{1,0:T(8,128)} %get-tuple-element.292), channel_id=1, source_target_pairs={{0,12},{4,0},{8,4},{12,8},{1,13},{5,1},{9,5},{13,9},{2,14},{6,2},{... | collective-permute-start | bytes 497672 | tf_op jit(solution)/shard_map/ppermute | solution.py:36
  615.8 21.0 %collective-permute-start.80 = (f32[4736]{0:T(1024)}, f32[4736]{0:T(1024)}, u32[]{:S(2)}, u32[]{:S(2)}) collective-permute-start(f32[4736]{0:T(1024)} %concatenate.162), channel_id=1, source_target_pairs={{0,16},{16,0},{1,17},{17,1},{2,18},{18,2},{3,19},{19,3},{4,20},{20... | collective-permute-start | bytes 56840 | tf_op jit(solution)/shard_map/ppermute | solution.py:54
  641.4 17.8 %collective-permute-start.88 = (f32[4,144,288]{2,1,0:T(8,128)S(1)}, f32[4,144,288]{2,1,0:T(8,128)S(1)}, u32[]{:S(2)}, u32[]{:S(2)}) collective-permute-start(f32[4,144,288]{2,1,0:T(8,128)S(1)} %pad_maximum_fusion.18), channel_id=1, source_target_pairs={{0,16},{16,0},{1,17},{17,1},{2,18},{18,2},{3,19},{19,3},{4,20},{20... | collective-permute-start | bytes 1990664 | tf_op jit(solution)/shard_map/ppermute | solution.py:54
  (130 other events, 1106.3 us)
Sparse Core Ops, SparseCore 0:
  110.8 51.5 all-gather.1
  420.2 93.6 reduce-scatter.1
where the time goes:
time: 679 us; the launch traced here: 671 us
  waiting for transfers between devices  239 us (35%)
  starting transfers between devices  152 us (22%)
  local copies, waits for them, and re-layouts  94.8 us (14%)
  matrix products  88.6 us (13%)
  other arithmetic  72.5 us (11%)
  between operations  17.7 us (3%)
    ppermute x42, starting transfers between devices, shift_row(): lax.ppermute(values, 'row', [(i, (i + step) % count) for i in range(count)])  101 us
    ppermute x42, waiting for transfers between devices, shift_row(): lax.ppermute(values, 'row', [(i, (i + step) % count) for i in range(count)])  91.8 us
    dot_general x30, matrix products, contract(): lax.dot_general(left, right, (((left_dim,), (right_dim,)), ((), ())), pre...  74.1 us
    ppermute x24, waiting for transfers between devices, shift_chip(): return lax.ppermute(values, 'col', pairs)  66.9 us
    ppermute x8, waiting for transfers between devices, swap_dp(): return lax.ppermute(values, 'dp', [(0, 1), (1, 0)])  51.4 us
    unnamed x234, local copies, waits for them, and re-layouts  33.5 us
    ppermute x8, waiting for transfers between devices, butterfly(): lax.ppermute(values, axis, [(i, i ^ step) for i in range(count)])  23 us
    ppermute x24, starting transfers between devices, shift_chip(): return lax.ppermute(values, 'col', pairs)  21.6 us
  transfers between devices with their start and end apart: 96, of which 41 were waited for; matrix products, arithmetic and copies ran while one was open for 34% of the time, Pallas kernels for 1%

commit v1 on v0

--- a/solution.py
+++ b/solution.py
@@ -68,25 +68,26 @@
     return sorted(range(count), key=lambda step: (min(step, count - step), step))
 
 
-def spread(block, ready=()):
+def spread(block, ready_chip=(), ready_core=()):
     count = lax.axis_size("row")
     chips = lax.axis_size("col") // 2
     by_step = {0: block}
     own_chips = [shift_chip(block, chip) for chip in range(chips)]
+    last = row_order()[-1]
     for step in row_order()[1:-1]:
         if step <= count // 2:
             by_step[step] = shift_row(by_step[step - 1], 1)
         else:
             by_step[step] = shift_row(by_step[(step + 1) % count], -1)
-    by_step, ready = lax.optimization_barrier((by_step, ready))
-    last = row_order()[-1]
-    by_step[last] = shift_row(by_step[last - 1], 1)
+    far = shift_row(by_step[last - 1], 1)
+    by_step, ready_chip = lax.optimization_barrier((by_step, ready_chip))
     groups = [own_chips]
-    for step in row_order()[1:]:
+    for step in row_order()[1:-1]:
         groups.append([shift_chip(by_step[step], chip) for chip in range(chips)])
-    near = jnp.concatenate(sum(groups[:-1], []), axis=0)
-    far = jnp.concatenate(groups[-1], axis=0)
-    return [near, far, swap_core(near), swap_core(far)], ready
+    far = jnp.concatenate([shift_chip(far, chip) for chip in range(chips)], axis=0)
+    near = jnp.concatenate(sum(groups, []), axis=0)
+    near, ready_core = lax.optimization_barrier((near, ready_core))
+    return [near, far, swap_core(near), swap_core(far)], ready_chip, ready_core
 
 
 def by_piece(function, pieces):
@@ -326,8 +327,9 @@
     both_own = by_source(both_own)
     in_own = jnp.concatenate([part[:, :width_row] for part in both_own], axis=1)
     cot_own = jnp.concatenate([part[:, width_row:] for part in both_own], axis=1)
+    normed_one, inverse_one = normalize(in_own)
     silu_now, qkv_now, out_now, up_now, down_now = after(
-        (silu_cond, w_qkv, w_out, w_up, w_down), in_own
+        (silu_cond, w_qkv, w_out, w_up, w_down), normed_one
     )
     ada_terms = jnp.sum(silu_now[0][:, None, None] * w_ada, axis=0)
 
@@ -355,7 +357,7 @@
         1,
     )
     mlp_sent = row_outgoing(mlp_blocks)
-    in_pieces, mlp_sent = spread(in_own, mlp_sent)
+    in_pieces, _, mlp_sent = spread(normed_one, (), mlp_sent)
     ada_terms = butterfly(ada_terms, "col") + b_ada
     head_blocks = move_rows(head_blocks)
     mlp_blocks = row_major(jnp.stack(row_send(mlp_sent)))
@@ -369,8 +371,7 @@
     head_matrix = jnp.concatenate(order_blocks(after(head_blocks, in_pieces[1])), axis=0)
     qkv_matrix = head_matrix[:, : 3 * head_width]
     out_flip = head_matrix[:, 3 * head_width :]
-    normed_one, inverse_one = normalize(in_own)
-    hidden_one = [normalize(piece)[0] * (1.0 + scale_one) + shift_one for piece in in_pieces]
+    hidden_one = [piece * (1.0 + scale_one) + shift_one for piece in in_pieces]
     head_start = (me_row // copies) * head_width
     head_bias = lax.dynamic_slice_in_dim(b_qv, head_start, head_width, 1)
     qkv = by_piece(lambda piece: contract(piece, qkv_matrix, 1, 0), hidden_one)
@@ -408,7 +409,7 @@
     cot_all = gather_mesh(after(cot_own, in_pieces[1]))
     d_activated = contract(cot_all, gate_two.reshape(width, 1) * down_matrix, 1, 0)
     d_activated = take_blocks(d_activated, tokens_mesh)
-    hidden_two, (up_matrix, down_matrix, d_activated) = spread(
+    hidden_two, (up_matrix, down_matrix, d_activated), _ = spread(
         hidden_two_own, (up_matrix, down_matrix, d_activated)
     )
     up_bias = lax.dynamic_slice_in_dim(b_up, me_row * units_own, units_own, 0)
@@ -418,18 +419,19 @@
 
     def mlp_rest(earlier):
         activated_mesh = take_blocks(after(activated, earlier), mesh_tokens)
-        up_grad = contract(jnp.concatenate(after(hidden_two, earlier)), d_up, 0, 0)
-        down_grad = contract(cot_all, activated_mesh, 0, 0) * gate_two.reshape(width, 1)
-        halves = pair_halves(jnp.concatenate([up_grad, down_grad], axis=1))
-        return contract(activated_mesh, down_matrix, 1, 1), halves
-
-    d_hidden_two, mlp_rest_done = scatter_tokens(
+        return activated_mesh, contract(activated_mesh, down_matrix, 1, 1)
+
+    d_hidden_two, (activated_mesh, mlp_part) = scatter_tokens(
         lambda start, size: contract(d_up[start : start + size], up_matrix, 1, 1), tokens, mlp_rest
     )
 
     d_mixed = cot_own + normalize_back(d_hidden_two * (1.0 + scale_two), normed_two, inverse_two)
     d_attn_own = d_mixed * gate_one
-    d_attn, (mlp_part, (mlp_kept, mlp_given)) = spread(d_attn_own, mlp_rest_done)
+    units = after((hidden_two, d_up, cot_all, activated_mesh), d_attn_own)
+    up_grad = contract(jnp.concatenate(units[0]), units[1], 0, 0)
+    down_grad = contract(units[2], units[3], 0, 0) * gate_two.reshape(width, 1)
+    mlp_halves = pair_halves(jnp.concatenate([up_grad, down_grad], axis=1))
+    d_attn, mlp_part, (mlp_kept, mlp_given) = spread(d_attn_own, mlp_part, mlp_halves)
     mlp_own = scatter_mesh(mlp_part)
     mlp_given = pair_swap(mlp_given)
     d_attended = by_piece(lambda piece: contract(piece, out_flip, 1, 0), d_attn)
@@ -456,9 +458,10 @@
 
     def head_rest_row(earlier, filled):
         mlp_moved, kept, given = filled
-        return share_blocks(after(mlp_moved, earlier)), kept, given
-
-    d_hidden_one, (mlp_shared, head_kept, head_given) = scatter_tokens(
+        mlp_shared = share_blocks(after(mlp_moved, earlier))
+        return mlp_shared, move_rows(after(kept + given, earlier))
+
+    d_hidden_one, (mlp_shared, head_moved) = scatter_tokens(
         lambda start, size: contract(d_qkv[start : start + size], qkv_matrix, 1, 1)
         * (1.0 / copies),
         tokens,
@@ -482,7 +485,6 @@
             for i in range(rows)
         ]
     )
-    results = row_parts(results)
 
     unit_sums = jnp.concatenate([jnp.sum(d_up, axis=0), jnp.sum(d_qkv, axis=0)])
     unit_sums = jnp.stack(by_source([shift_row(unit_sums, step) for step in range(rows)]))
@@ -498,11 +500,11 @@
             jnp.sum(d_mlp_own, axis=0),
         ]
     )
+    results = row_parts(results)
     own_sums = butterfly(own_sums, "col")
-    head_kept, head_given = after((head_kept, head_given), own_sums)
-    head_moved = move_rows(head_kept + head_given)
     own_sums = butterfly(own_sums, "row")
-    head_grad = order_blocks(share_blocks(after(head_moved, own_sums)))[::copies]
+    head_grad = share_blocks(after(head_moved, d_hidden_one))
+    head_grad = order_blocks(after(head_grad, own_sums))[::copies]
     qkv_grad = jnp.stack(
         [part[:, : 3 * head_width].reshape(width_row, 3, head_width) for part in head_grad],
         axis=2,
@@ -512,7 +514,6 @@
     up_grad = jnp.concatenate([part[:, :units_own] for part in mlp_grad], axis=1)
     down_grad = jnp.concatenate([part[:, units_own:].T for part in mlp_grad], axis=0)
     own_sums = lax.dynamic_slice_in_dim(own_sums, me_row * width_row, width_row, 1)
-    results = jnp.concatenate(by_source(after(results, own_sums)), axis=0)
     label_row = jnp.broadcast_to(labels.astype(jnp.float32), (128,))
     unit_size = unit_sums.size
     pack = dp_stack(
@@ -530,6 +531,7 @@
     silu_grads = butterfly(silu_grads, "row")
     (cond_grad,) = silu_pull(silu_grads)
     cond_all = dp_stack(cond_grad[0])
+    results = jnp.concatenate(by_source(after(results, cond_all)), axis=0)
     label_all = pack[:, -1].astype(jnp.int32)
     classes = jnp.arange(class_table.shape[0])
     table_grad = jnp.sum(

time: 679 us -> 645 us (0.950)
  waiting for transfers between devices: 239 us -> 217 us
  other arithmetic: 72.5 us -> 60.7 us
    ppermute x8, waiting for transfers between devices: 51.4 us -> 21.2 us  [swap_dp(): return lax.ppermute(values, 'dp', [(0, 1), (1, 0)])]
    ppermute x42, waiting for transfers between devices: 91.8 us -> 107 us  [shift_row(): lax.ppermute(values, 'row', [(i, (i + step) % count) for i in range(count)])]
    ppermute x8, waiting for transfers between devices: 23 us -> 9.4 us  [butterfly(): lax.ppermute(values, axis, [(i, i ^ step) for i in range(count)])]
    ppermute x24, starting transfers between devices: 21.6 us -> 30.6 us  [shift_chip(): return lax.ppermute(values, 'col', pairs)]
    reduce_sum x7 -> x1, other arithmetic: 9.53 us -> 0.89 us  [normalize(): center = jnp.mean(values, axis=1, keepdims=True)]
    unnamed x234 -> x236, local copies, waits for them, and re-layouts: 33.5 us -> 34.4 us
  transfers between devices with their start and end apart: 96 -> 96, of which waited for: 41 -> 36; matrix products, arithmetic and copies ran while one was open for 34% -> 34% of each run, Pallas kernels for 1% -> 1%
where the time goes in v1:
time: 645 us; the launch traced here: 637 us
  waiting for transfers between devices  217 us (34%)
  starting transfers between devices  150 us (23%)
  local copies, waits for them, and re-layouts  97.1 us (15%)
  matrix products  88.2 us (14%)
  other arithmetic  60.7 us (9%)
  between operations  17.5 us (3%)
    ppermute x42, waiting for transfers between devices, shift_row(): lax.ppermute(values, 'row', [(i, (i + step) % count) for i in range(count)])  107 us
    ppermute x42, starting transfers between devices, shift_row(): lax.ppermute(values, 'row', [(i, (i + step) % count) for i in range(count)])  95.4 us
    dot_general x30, matrix products, contract(): lax.dot_general(left, right, (((left_dim,), (right_dim,)), ((), ())), pre...  73.7 us
    ppermute x24, waiting for transfers between devices, shift_chip(): return lax.ppermute(values, 'col', pairs)  73.4 us
    unnamed x236, local copies, waits for them, and re-layouts  34.4 us
    ppermute x24, starting transfers between devices, shift_chip(): return lax.ppermute(values, 'col', pairs)  30.6 us
    ppermute x8, waiting for transfers between devices, swap_dp(): return lax.ppermute(values, 'dp', [(0, 1), (1, 0)])  21.2 us
    ppermute x8, starting transfers between devices, butterfly(): lax.ppermute(values, axis, [(i, i ^ step) for i in range(count)])  13 us
  transfers between devices with their start and end apart: 96, of which 36 were waited for; matrix products, arithmetic and copies ran while one was open for 34% of the time, Pallas kernels for 1%

profile of v1, /device:TPU:0, one launch (start us, length us, event | category | flops | bytes accessed | tf_op | source)
XLA Modules:
  0.0 637.1 jit_solution(11915419798348408041)
XLA Ops:
  9.9 5.1 collective-permute-start.2
  21.2 7.7 %collective-permute-done.1 = f32[64,576]{1,0:T(8,128)S(1)} collective-permute-done((f32[64,576]{1,0:T(8,128)S(1)}, f32[64,576]{1,0:T(8,128)S(1)}, u32[]{:S(2)}, u32[]{:S(2)}) %collective-permute-start.1) | collective-permute-done | bytes 147488 | tf_op jit(solution)/shard_map/ppermute | solution.py:36
  51.1 2.3 collective-permute-start.16
  55.5 9.4 %collective-permute-done.16 = f32[144,288]{1,0:T(8,128)S(1)} collective-permute-done((f32[144,288]{1,0:T(8,128)S(1)}, f32[144,288]{1,0:T(8,128)S(1)}, u32[]{:S(2)}, u32[]{:S(2)}) %collective-permute-start.16) | collective-permute-done | bytes 165920 | tf_op jit(solution)/shard_map/ppermute | solution.py:36
  64.9 5.9 collective-permute-start.7
  77.9 4.7 collective-permute-done.13
  93.2 4.9 collective-permute-done.10
  106.7 2.3 multiply_add_fusion.1
  111.7 2.3 fusion.17
  118.6 3.4 collective-permute-done.26
  123.7 14.7 %collective-permute-done.27 = f32[64,1152]{1,0:T(8,128)S(1)} collective-permute-done((f32[64,1152]{1,0:T(8,128)S(1)}, f32[64,1152]{1,0:T(8,128)S(1)}, u32[]{:S(2)}, u32[]{:S(2)}) %collective-permute-start.27) | collective-permute-done | bytes 294944 | tf_op jit(solution)/shard_map/ppermute | solution.py:46
  144.1 21.0 %collective-permute-done.28 = f32[64,1152]{1,0:T(8,128)S(1)} collective-permute-done((f32[64,1152]{1,0:T(8,128)S(1)}, f32[64,1152]{1,0:T(8,128)S(1)}, u32[]{:S(2)}, u32[]{:S(2)}) %collective-permute-start.28) | collective-permute-done | bytes 294944 | tf_op jit(solution)/shard_map/ppermute | solution.py:36
  170.3 13.9 %collective-permute-done.33 = f32[144,576]{1,0:T(8,128)S(1)} collective-permute-done((f32[144,576]{1,0:T(8,128)S(1)}, f32[144,576]{1,0:T(8,128)S(1)}, u32[]{:S(2)}, u32[]{:S(2)}) %collective-permute-start.33) | collective-permute-done | bytes 331808 | tf_op jit(solution)/shard_map/ppermute | solution.py:36
  184.2 4.9 collective-permute-done.34
  189.4 3.0 collective-permute-done.29
  194.9 6.6 %collective-permute-start.30 = (f32[64,1152]{1,0:T(8,128)}, f32[64,1152]{1,0:T(8,128)}, u32[]{:S(2)}, u32[]{:S(2)}) collective-permute-start(f32[64,1152]{1,0:T(8,128)} %get-tuple-element.204), channel_id=1, source_target_pairs={{0,4},{4,8},{8,12},{12,0},{1,5},{5,9},{9,13},{13,1},{2,6},{6,10},{... | collective-permute-start | bytes 884744 | tf_op jit(solution)/shard_map/ppermute | solution.py:36
  203.9 5.3 collective-permute-done.30
  209.2 7.9 %collective-permute-start.39 = (f32[64,1152]{1,0:T(8,128)}, f32[64,1152]{1,0:T(8,128)}, u32[]{:S(2)}, u32[]{:S(2)}) collective-permute-start(f32[64,1152]{1,0:T(8,128)} %collective-permute-done.30), channel_id=1, source_target_pairs={{0,4},{4,8},{8,12},{12,0},{1,5},{5,9},{9,13},{13,1},{2,6},{6,10},{... | collective-permute-start | bytes 884744 | tf_op jit(solution)/shard_map/ppermute | solution.py:36
  225.2 3.8 fusion.155
  229.0 8.2 %fusion.18.source_ref = f32[1024,288]{1,0:T(8,128)} fusion(f32[1024,1152]{1,0:T(8,128)} %all-gather.2.cloned.1.call-done, f32[1152]{0:T(1024)S(1)} %get-tuple-element.179, f32[1152,576]{1,0:T(8,128)} %bitcast_dynamic-update-slice_fusion), kind=kOutput, calls=%fused_computation.48 | convolution fusion | flops 2038763520 | bytes 7672320 | tf_op jit(solution)/shard_map/dot_general | solution.py:19
  237.2 3.2 take_blocks.2
  240.4 5.8 collective-permute-start.37
  249.6 3.9 collective-permute-done.37
  260.8 6.2 collective-permute-done.40
  274.0 3.2 fusion.172
  277.3 2.9 fusion.145
  283.6 3.1 collective-permute-done.48
  289.5 7.6 %collective-permute-done.49 = f32[64,1152]{1,0:T(8,128)S(1)} collective-permute-done((f32[64,1152]{1,0:T(8,128)S(1)}, f32[64,1152]{1,0:T(8,128)S(1)}, u32[]{:S(2)}, u32[]{:S(2)}) %collective-permute-start.49) | collective-permute-done | bytes 294944 | tf_op jit(solution)/shard_map/ppermute | solution.py:46
  297.8 11.6 %collective-permute-start.50 = (f32[64,1152]{1,0:T(8,128)}, f32[64,1152]{1,0:T(8,128)}, u32[]{:S(2)}, u32[]{:S(2)}) collective-permute-start(f32[64,1152]{1,0:T(8,128)} %slice_add_fusion.4), channel_id=1, source_target_pairs={{0,12},{4,0},{8,4},{12,8},{1,13},{5,1},{9,5},{13,9},{2,14},{6,2},{... | collective-permute-start | bytes 884744 | tf_op jit(solution)/shard_map/ppermute | solution.py:36
  317.7 2.9 take_blocks.3
  320.5 2.9 collective-permute-done.47
  323.4 6.3 collective-permute-done.45
  332.0 3.8 collective-permute-start.51
  335.8 7.1 %fusion.174 = f32[1024,1152]{1,0:T(8,128)} fusion(f32[1024,288]{1,0:T(8,128)S(1)} %copy-done.2, f32[1152,288]{1,0:T(8,128)} %get-tuple-element.95), kind=kOutput, calls=%fused_computation.482 | convolution fusion | flops 2038431744 | bytes 7225344 | tf_op jit(solution)/shard_map/dot_general | solution.py:19
  351.7 6.3 convolution_multiply_fusion
  358.1 5.8 fusion
  369.5 4.8 collective-permute-done.55
  374.3 3.1 collective-permute-done.56
  380.0 6.9 %collective-permute-done.58 = f32[64,1152]{1,0:T(8,128)S(1)} collective-permute-done((f32[64,1152]{1,0:T(8,128)S(1)}, f32[64,1152]{1,0:T(8,128)S(1)}, u32[]{:S(2)}, u32[]{:S(2)}) %collective-permute-start.58) | collective-permute-done | bytes 294944 | tf_op jit(solution)/shard_map/ppermute | solution.py:46
  393.6 2.8 fusion.58
  398.7 2.6 multiply_reduce_fusion.1
  401.4 2.8 fusion.29
  404.2 2.7 fusion.28
  410.5 3.0 fusion.34
  415.6 3.0 collective-permute-start.82
  418.7 2.8 constant_dynamic-update-slice_fusion.25
  431.7 5.7 collective-permute-done.67
  438.2 3.3 collective-permute-start.68
  441.4 3.3 convolution_add_fusion
  449.2 3.7 fusion.175
  459.3 2.5 collective-permute-start.92
  465.8 2.5 collective-permute-start.69
  468.4 15.3 %collective-permute-done.91 = f32[144,576]{1,0:T(8,128)} collective-permute-done((f32[144,576]{1,0:T(8,128)}, f32[144,576]{1,0:T(8,128)}, u32[]{:S(2)}, u32[]{:S(2)}) %collective-permute-start.91) | collective-permute-done | bytes 331808 | tf_op jit(solution)/shard_map/ppermute | solution.py:36
  483.7 16.1 %collective-permute-start.64 = (f32[64,1152]{1,0:T(8,128)}, f32[64,1152]{1,0:T(8,128)}, u32[]{:S(2)}, u32[]{:S(2)}) collective-permute-start(f32[64,1152]{1,0:T(8,128)} %get-tuple-element.245), channel_id=1, source_target_pairs={{0,4},{4,8},{8,12},{12,0},{1,5},{5,9},{9,13},{13,1},{2,6},{6,10},{... | collective-permute-start | bytes 884744 | tf_op jit(solution)/shard_map/ppermute | solution.py:36
  504.9 5.3 collective-permute-done.64
  513.6 2.3 collective-permute-start.85
  517.5 12.2 %collective-permute-done.86 = f32[144,288]{1,0:T(8,128)S(1)} collective-permute-done((f32[144,288]{1,0:T(8,128)S(1)}, f32[144,288]{1,0:T(8,128)S(1)}, u32[]{:S(2)}, u32[]{:S(2)}) %collective-permute-start.86) | collective-permute-done | bytes 165920 | tf_op jit(solution)/shard_map/ppermute | solution.py:36
  535.0 21.2 %collective-permute-done.88 = f32[4,144,288]{2,1,0:T(8,128)S(1)} collective-permute-done((f32[4,144,288]{2,1,0:T(8,128)S(1)}, f32[4,144,288]{2,1,0:T(8,128)S(1)}, u32[]{:S(2)}, u32[]{:S(2)}) %collective-permute-start.88) | collective-permute-done | bytes 663584 | tf_op jit(solution)/shard_map/ppermute | solution.py:54
  564.5 3.2 collective-permute-done.74
  568.1 3.6 collective-permute-done.75
  571.7 3.5 collective-permute-start.76
  582.7 3.8 collective-permute-start.77
  605.7 4.0 collective-permute-start.78
  615.4 2.4 concatenate.176
  (611 shorter events, 251.3 us)
Async XLA Ops:
  7.2 221.8 %all-gather.2.cloned.1.call-start = ((), (), s32[]{:S(2)}) async-start(), calls=%async_computation.1 | async-start | bytes 5013504 | tf_op jit(solution)/shard_map/all_gather | solution.py:174
  15.1 13.9 %collective-permute-start.1 = (f32[64,576]{1,0:T(8,128)S(1)}, f32[64,576]{1,0:T(8,128)S(1)}, u32[]{:S(2)}, u32[]{:S(2)}) collective-permute-start(f32[64,576]{1,0:T(8,128)S(1)} %get-tuple-element.331), channel_id=1, source_target_pairs={{0,8},{4,12},{8,0},{12,4},{1,9},{5,13},{9,1},{13,5},{2,10},{6,14},... | collective-permute-start | bytes 442376 | tf_op jit(solution)/shard_map/ppermute | solution.py:36
  15.1 13.9 %collective-permute-start = (f32[64,576]{1,0:T(8,128)S(1)}, f32[64,576]{1,0:T(8,128)S(1)}, u32[]{:S(2)}, u32[]{:S(2)}) collective-permute-start(f32[64,576]{1,0:T(8,128)S(1)} %get-tuple-element.332), channel_id=1, source_target_pairs={{0,4},{4,8},{8,12},{12,0},{1,5},{5,9},{9,13},{13,1},{2,6},{6,10},{... | collective-permute-start | bytes 442376 | tf_op jit(solution)/shard_map/ppermute | solution.py:36
  33.6 37.3 %collective-permute-start.12 = (f32[64,1152]{1,0:T(8,128)S(1)}, f32[64,1152]{1,0:T(8,128)}, u32[]{:S(2)}, u32[]{:S(2)}) collective-permute-start(f32[64,1152]{1,0:T(8,128)S(1)} %get-tuple-element.209), channel_id=1, source_target_pairs={{0,12},{4,0},{8,4},{12,8},{1,13},{5,1},{9,5},{13,9},{2,14},{6,2},{... | collective-permute-start | bytes 884744 | tf_op jit(solution)/shard_map/ppermute | solution.py:36
  34.6 38.8 %collective-permute-start.11 = (f32[64,1152]{1,0:T(8,128)S(1)}, f32[64,1152]{1,0:T(8,128)}, u32[]{:S(2)}, u32[]{:S(2)}) collective-permute-start(f32[64,1152]{1,0:T(8,128)S(1)} %get-tuple-element.209), channel_id=1, source_target_pairs={{0,2},{1,3},{2,0},{3,1},{4,6},{5,7},{6,4},{7,5},{8,10},{9,11},{10,... | collective-permute-start | bytes 884744 | tf_op jit(solution)/shard_map/ppermute | solution.py:46
  36.2 36.3 %collective-permute-start.8 = (f32[64,1152]{1,0:T(8,128)S(1)}, f32[64,1152]{1,0:T(8,128)}, u32[]{:S(2)}, u32[]{:S(2)}) collective-permute-start(f32[64,1152]{1,0:T(8,128)S(1)} %get-tuple-element.209), channel_id=1, source_target_pairs={{0,4},{4,8},{8,12},{12,0},{1,5},{5,9},{9,13},{13,1},{2,6},{6,10},{... | collective-permute-start | bytes 884744 | tf_op jit(solution)/shard_map/ppermute | solution.py:36
  51.1 13.8 %collective-permute-start.16 = (f32[144,288]{1,0:T(8,128)S(1)}, f32[144,288]{1,0:T(8,128)S(1)}, u32[]{:S(2)}, u32[]{:S(2)}) collective-permute-start(f32[144,288]{1,0:T(8,128)S(1)} %get-tuple-element.266), channel_id=1, source_target_pairs={{0,8},{4,12},{8,0},{12,4},{1,9},{5,13},{9,1},{13,5},{2,10},{6,14},... | collective-permute-start | bytes 497672 | tf_op jit(solution)/shard_map/ppermute | solution.py:36
  55.2 15.6 %collective-permute-start.17 = (f32[144,288]{1,0:T(8,128)S(1)}, f32[144,288]{1,0:T(8,128)S(1)}, u32[]{:S(2)}, u32[]{:S(2)}) collective-permute-start(f32[144,288]{1,0:T(8,128)S(1)} %get-tuple-element.267), channel_id=1, source_target_pairs={{0,12},{4,0},{8,4},{12,8},{1,13},{5,1},{9,5},{13,9},{2,14},{6,2},{... | collective-permute-start | bytes 497672 | tf_op jit(solution)/shard_map/ppermute | solution.py:36
  64.9 34.0 %collective-permute-start.7 = (f32[8,288]{1,0:T(8,128)S(1)}, f32[8,288]{1,0:T(8,128)S(1)}, u32[]{:S(2)}, u32[]{:S(2)}) collective-permute-start(f32[8,288]{1,0:T(8,128)S(1)} %pad_maximum_fusion.42), channel_id=1, source_target_pairs={{0,12},{4,0},{8,4},{12,8},{1,13},{5,1},{9,5},{13,9},{2,14},{6,2},{... | collective-permute-start | bytes 27656 | tf_op jit(solution)/shard_map/ppermute | solution.py:36
  70.8 28.1 %collective-permute-start.6 = (f32[8,288]{1,0:T(8,128)S(1)}, f32[8,288]{1,0:T(8,128)S(1)}, u32[]{:S(2)}, u32[]{:S(2)}) collective-permute-start(f32[8,288]{1,0:T(8,128)S(1)} %pad_maximum_fusion.42), channel_id=1, source_target_pairs={{0,8},{4,12},{8,0},{12,4},{1,9},{5,13},{9,1},{13,5},{2,10},{6,14},... | collective-permute-start | bytes 27656 | tf_op jit(solution)/shard_map/ppermute | solution.py:36
  70.9 22.2 %collective-permute-start.18 = (f32[4,144,288]{2,1,0:T(8,128)S(1)}, f32[4,144,288]{2,1,0:T(8,128)S(1)}, u32[]{:S(2)}, u32[]{:S(2)}) collective-permute-start(f32[4,144,288]{2,1,0:T(8,128)S(1)} %get-tuple-element.308), channel_id=1, source_target_pairs={{0,16},{16,0},{1,17},{17,1},{2,18},{18,2},{3,19},{19,3},{4,20},{20... | collective-permute-start | bytes 1990664 | tf_op jit(solution)/shard_map/ppermute | solution.py:54
  73.4 13.1 %collective-permute-start.14 = (f32[64,1152]{1,0:T(8,128)}, f32[64,1152]{1,0:T(8,128)S(1)}, u32[]{:S(2)}, u32[]{:S(2)}) collective-permute-start(f32[64,1152]{1,0:T(8,128)} %collective-permute-done.12), channel_id=1, source_target_pairs={{0,2},{1,3},{2,0},{3,1},{4,6},{5,7},{6,4},{7,5},{8,10},{9,11},{10,... | collective-permute-start | bytes 884744 | tf_op jit(solution)/shard_map/ppermute | solution.py:46
  93.1 13.6 %collective-permute-start.19 = (f32[384,1152]{1,0:T(8,128)}, f32[384,1152]{1,0:T(8,128)}, u32[]{:S(2)}, u32[]{:S(2)}) collective-permute-start(f32[384,1152]{1,0:T(8,128)} %constant_dynamic-update-slice_fusion.2), channel_id=1, source_target_pairs={{0,1},{1,0},{2,3},{3,2},{4,5},{5,4},{6,7},{7,6},{8,9},{9,8},{10,11... | collective-permute-start | bytes 5308424 | tf_op jit(solution)/shard_map/ppermute | solution.py:50
  99.6 458.2 %reduce-scatter.2.cloned.1.call-start = ((), (), s32[]{:S(2)}) async-start(), calls=%async_computation.2 | async-start | bytes 5013504 | tf_op jit(solution)/shard_map/reduce_scatter | solution.py:178
  117.3 21.4 %collective-permute-start.21 = (f32[384,1152]{1,0:T(8,128)S(1)}, f32[384,1152]{1,0:T(8,128)S(1)}, u32[]{:S(2)}, u32[]{:S(2)}) collective-permute-start(f32[384,1152]{1,0:T(8,128)S(1)} %fusion.67), channel_id=1, source_target_pairs={{0,1},{1,0},{2,3},{3,2},{4,5},{5,4},{6,7},{7,6},{8,9},{9,8},{10,11... | collective-permute-start | bytes 5308424 | tf_op jit(solution)/shard_map/ppermute | solution.py:50
  122.7 15.6 %collective-permute-start.27 = (f32[64,1152]{1,0:T(8,128)S(1)}, f32[64,1152]{1,0:T(8,128)S(1)}, u32[]{:S(2)}, u32[]{:S(2)}) collective-permute-start(f32[64,1152]{1,0:T(8,128)S(1)} %slice.537), channel_id=1, source_target_pairs={{0,2},{1,3},{2,0},{3,1},{4,6},{5,7},{6,4},{7,5},{8,10},{9,11},{10,... | collective-permute-start | bytes 884744 | tf_op jit(solution)/shard_map/ppermute | solution.py:46
  138.4 26.8 %collective-permute-start.28 = (f32[64,1152]{1,0:T(8,128)S(1)}, f32[64,1152]{1,0:T(8,128)S(1)}, u32[]{:S(2)}, u32[]{:S(2)}) collective-permute-start(f32[64,1152]{1,0:T(8,128)S(1)} %slice_add_fusion.8), channel_id=1, source_target_pairs={{0,12},{4,0},{8,4},{12,8},{1,13},{5,1},{9,5},{13,9},{2,14},{6,2},{... | collective-permute-start | bytes 884744 | tf_op jit(solution)/shard_map/ppermute | solution.py:36
  140.0 25.2 %collective-permute-start.25 = (f32[64,1152]{1,0:T(8,128)S(1)}, f32[64,1152]{1,0:T(8,128)S(1)}, u32[]{:S(2)}, u32[]{:S(2)}) collective-permute-start(f32[64,1152]{1,0:T(8,128)S(1)} %get-tuple-element.252), channel_id=1, source_target_pairs={{0,2},{1,3},{2,0},{3,1},{4,6},{5,7},{6,4},{7,5},{8,10},{9,11},{10,... | collective-permute-start | bytes 884744 | tf_op jit(solution)/shard_map/ppermute | solution.py:46
  141.2 25.1 %collective-permute-start.23 = (f32[64,1152]{1,0:T(8,128)S(1)}, f32[64,1152]{1,0:T(8,128)S(1)}, u32[]{:S(2)}, u32[]{:S(2)}) collective-permute-start(f32[64,1152]{1,0:T(8,128)S(1)} %get-tuple-element.253), channel_id=1, source_target_pairs={{0,2},{1,3},{2,0},{3,1},{4,6},{5,7},{6,4},{7,5},{8,10},{9,11},{10,... | collective-permute-start | bytes 884744 | tf_op jit(solution)/shard_map/ppermute | solution.py:46
  142.1 26.3 %collective-permute-start.32 = (f32[144,576]{1,0:T(8,128)S(1)}, f32[144,576]{1,0:T(8,128)S(1)}, u32[]{:S(2)}, u32[]{:S(2)}) collective-permute-start(f32[144,576]{1,0:T(8,128)S(1)} %copy-done.64), channel_id=1, source_target_pairs={{0,4},{4,8},{8,12},{12,0},{1,5},{5,9},{9,13},{13,1},{2,6},{6,10},{... | collective-permute-start | bytes 995336 | tf_op jit(solution)/shard_map/ppermute | solution.py:36
  144.1 40.1 %collective-permute-start.33 = (f32[144,576]{1,0:T(8,128)S(1)}, f32[144,576]{1,0:T(8,128)S(1)}, u32[]{:S(2)}, u32[]{:S(2)}) collective-permute-start(f32[144,576]{1,0:T(8,128)S(1)} %copy-done.63), channel_id=1, source_target_pairs={{0,8},{4,12},{8,0},{12,4},{1,9},{5,13},{9,1},{13,5},{2,10},{6,14},... | collective-permute-start | bytes 995336 | tf_op jit(solution)/shard_map/ppermute | solution.py:36
  165.1 24.0 %collective-permute-start.34 = (f32[144,576]{1,0:T(8,128)S(1)}, f32[144,576]{1,0:T(8,128)S(1)}, u32[]{:S(2)}, u32[]{:S(2)}) collective-permute-start(f32[144,576]{1,0:T(8,128)S(1)} %copy-done.62), channel_id=1, source_target_pairs={{0,12},{4,0},{8,4},{12,8},{1,13},{5,1},{9,5},{13,9},{2,14},{6,2},{... | collective-permute-start | bytes 995336 | tf_op jit(solution)/shard_map/ppermute | solution.py:36
  165.1 24.2 %collective-permute-start.22 = (f32[64,1152]{1,0:T(8,128)S(1)}, f32[64,1152]{1,0:T(8,128)S(1)}, u32[]{:S(2)}, u32[]{:S(2)}) collective-permute-start(f32[64,1152]{1,0:T(8,128)S(1)} %get-tuple-element.251), channel_id=1, source_target_pairs={{0,2},{1,3},{2,0},{3,1},{4,6},{5,7},{6,4},{7,5},{8,10},{9,11},{10,... | collective-permute-start | bytes 884744 | tf_op jit(solution)/shard_map/ppermute | solution.py:46
  166.4 23.0 %collective-permute-start.24 = (f32[64,1152]{1,0:T(8,128)S(1)}, f32[64,1152]{1,0:T(8,128)S(1)}, u32[]{:S(2)}, u32[]{:S(2)}) collective-permute-start(f32[64,1152]{1,0:T(8,128)S(1)} %get-tuple-element.254), channel_id=1, source_target_pairs={{0,4},{4,8},{8,12},{12,0},{1,5},{5,9},{9,13},{13,1},{2,6},{6,10},{... | collective-permute-start | bytes 884744 | tf_op jit(solution)/shard_map/ppermute | solution.py:36
  168.4 23.9 %collective-permute-start.29 = (f32[64,1152]{1,0:T(8,128)S(1)}, f32[64,1152]{1,0:T(8,128)S(1)}, u32[]{:S(2)}, u32[]{:S(2)}) collective-permute-start(f32[64,1152]{1,0:T(8,128)S(1)} %get-tuple-element.255), channel_id=1, source_target_pairs={{0,12},{4,0},{8,4},{12,8},{1,13},{5,1},{9,5},{13,9},{2,14},{6,2},{... | collective-permute-start | bytes 884744 | tf_op jit(solution)/shard_map/ppermute | solution.py:36
  189.3 27.8 %collective-permute-start.35 = (f32[4,144,576]{2,1,0:T(8,128)S(1)}, f32[4,144,576]{2,1,0:T(8,128)}, u32[]{:S(2)}, u32[]{:S(2)}) collective-permute-start(f32[4,144,576]{2,1,0:T(8,128)S(1)} %pad_maximum_fusion.6), channel_id=1, source_target_pairs={{0,16},{16,0},{1,17},{17,1},{2,18},{18,2},{3,19},{19,3},{4,20},{20... | collective-permute-start | bytes 3981320 | tf_op jit(solution)/shard_map/ppermute | solution.py:54
  194.9 14.3 %collective-permute-start.30 = (f32[64,1152]{1,0:T(8,128)}, f32[64,1152]{1,0:T(8,128)}, u32[]{:S(2)}, u32[]{:S(2)}) collective-permute-start(f32[64,1152]{1,0:T(8,128)} %get-tuple-element.204), channel_id=1, source_target_pairs={{0,4},{4,8},{8,12},{12,0},{1,5},{5,9},{9,13},{13,1},{2,6},{6,10},{... | collective-permute-start | bytes 884744 | tf_op jit(solution)/shard_map/ppermute | solution.py:36
  202.1 44.1 %collective-permute-start.36 = (f32[64,1152]{1,0:T(8,128)}, f32[64,1152]{1,0:T(8,128)}, u32[]{:S(2)}, u32[]{:S(2)}) collective-permute-start(f32[64,1152]{1,0:T(8,128)} %get-tuple-element.204), channel_id=1, source_target_pairs={{0,2},{1,3},{2,0},{3,1},{4,6},{5,7},{6,4},{7,5},{8,10},{9,11},{10,... | collective-permute-start | bytes 884744 | tf_op jit(solution)/shard_map/ppermute | solution.py:46
  203.9 36.5 %collective-permute-start.31 = (f32[64,1152]{1,0:T(8,128)}, f32[64,1152]{1,0:T(8,128)}, u32[]{:S(2)}, u32[]{:S(2)}) collective-permute-start(f32[64,1152]{1,0:T(8,128)} %get-tuple-element.204), channel_id=1, source_target_pairs={{0,12},{4,0},{8,4},{12,8},{1,13},{5,1},{9,5},{13,9},{2,14},{6,2},{... | collective-permute-start | bytes 884744 | tf_op jit(solution)/shard_map/ppermute | solution.py:36
  209.2 48.2 %collective-permute-start.39 = (f32[64,1152]{1,0:T(8,128)}, f32[64,1152]{1,0:T(8,128)}, u32[]{:S(2)}, u32[]{:S(2)}) collective-permute-start(f32[64,1152]{1,0:T(8,128)} %collective-permute-done.30), channel_id=1, source_target_pairs={{0,4},{4,8},{8,12},{12,0},{1,5},{5,9},{9,13},{13,1},{2,6},{6,10},{... | collective-permute-start | bytes 884744 | tf_op jit(solution)/shard_map/ppermute | solution.py:36
  240.4 13.1 %collective-permute-start.37 = (f32[64,1152]{1,0:T(8,128)}, f32[64,1152]{1,0:T(8,128)S(1)}, u32[]{:S(2)}, u32[]{:S(2)}) collective-permute-start(f32[64,1152]{1,0:T(8,128)} %collective-permute-done.30), channel_id=1, source_target_pairs={{0,2},{1,3},{2,0},{3,1},{4,6},{5,7},{6,4},{7,5},{8,10},{9,11},{10,... | collective-permute-start | bytes 884744 | tf_op jit(solution)/shard_map/ppermute | solution.py:46
  257.4 16.6 %collective-permute-start.41 = (f32[384,1152]{1,0:T(8,128)}, f32[384,1152]{1,0:T(8,128)}, u32[]{:S(2)}, u32[]{:S(2)}) collective-permute-start(f32[384,1152]{1,0:T(8,128)} %constant_dynamic-update-slice_fusion.8), channel_id=1, source_target_pairs={{0,1},{1,0},{2,3},{3,2},{4,5},{5,4},{6,7},{7,6},{8,9},{9,8},{10,11... | collective-permute-start | bytes 5308424 | tf_op jit(solution)/shard_map/ppermute | solution.py:50
  281.9 27.5 %collective-permute-start.43 = (f32[384,1152]{1,0:T(8,128)S(1)}, f32[384,1152]{1,0:T(8,128)S(1)}, u32[]{:S(2)}, u32[]{:S(2)}) collective-permute-start(f32[384,1152]{1,0:T(8,128)S(1)} %fusion.45), channel_id=1, source_target_pairs={{0,1},{1,0},{2,3},{3,2},{4,5},{5,4},{6,7},{7,6},{8,9},{9,8},{10,11... | collective-permute-start | bytes 5308424 | tf_op jit(solution)/shard_map/ppermute | solution.py:50
  297.8 22.7 %collective-permute-start.50 = (f32[64,1152]{1,0:T(8,128)}, f32[64,1152]{1,0:T(8,128)}, u32[]{:S(2)}, u32[]{:S(2)}) collective-permute-start(f32[64,1152]{1,0:T(8,128)} %slice_add_fusion.4), channel_id=1, source_target_pairs={{0,12},{4,0},{8,4},{12,8},{1,13},{5,1},{9,5},{13,9},{2,14},{6,2},{... | collective-permute-start | bytes 884744 | tf_op jit(solution)/shard_map/ppermute | solution.py:36
  315.0 14.8 %collective-permute-start.45 = (f32[64,1152]{1,0:T(8,128)}, f32[64,1152]{1,0:T(8,128)}, u32[]{:S(2)}, u32[]{:S(2)}) collective-permute-start(f32[64,1152]{1,0:T(8,128)} %get-tuple-element.248), channel_id=1, source_target_pairs={{0,2},{1,3},{2,0},{3,1},{4,6},{5,7},{6,4},{7,5},{8,10},{9,11},{10,... | collective-permute-start | bytes 884744 | tf_op jit(solution)/shard_map/ppermute | solution.py:46
  315.9 27.0 %collective-permute-start.44 = (f32[64,1152]{1,0:T(8,128)}, f32[64,1152]{1,0:T(8,128)}, u32[]{:S(2)}, u32[]{:S(2)}) collective-permute-start(f32[64,1152]{1,0:T(8,128)} %get-tuple-element.246), channel_id=1, source_target_pairs={{0,2},{1,3},{2,0},{3,1},{4,6},{5,7},{6,4},{7,5},{8,10},{9,11},{10,... | collective-permute-start | bytes 884744 | tf_op jit(solution)/shard_map/ppermute | solution.py:46
  347.9 21.5 %collective-permute-start.54 = (f32[64,1152]{1,0:T(8,128)S(1)}, f32[64,1152]{1,0:T(8,128)S(1)}, u32[]{:S(2)}, u32[]{:S(2)}) collective-permute-start(f32[64,1152]{1,0:T(8,128)S(1)} %get-tuple-element.197), channel_id=1, source_target_pairs={{0,2},{1,3},{2,0},{3,1},{4,6},{5,7},{6,4},{7,5},{8,10},{9,11},{10,... | collective-permute-start | bytes 884744 | tf_op jit(solution)/shard_map/ppermute | solution.py:46
  349.6 16.7 %collective-permute-start.53 = (f32[64,1152]{1,0:T(8,128)S(1)}, f32[64,1152]{1,0:T(8,128)S(1)}, u32[]{:S(2)}, u32[]{:S(2)}) collective-permute-start(f32[64,1152]{1,0:T(8,128)S(1)} %get-tuple-element.197), channel_id=1, source_target_pairs={{0,12},{4,0},{8,4},{12,8},{1,13},{5,1},{9,5},{13,9},{2,14},{6,2},{... | collective-permute-start | bytes 884744 | tf_op jit(solution)/shard_map/ppermute | solution.py:36
  351.7 14.6 %collective-permute-start.52 = (f32[64,1152]{1,0:T(8,128)S(1)}, f32[64,1152]{1,0:T(8,128)S(1)}, u32[]{:S(2)}, u32[]{:S(2)}) collective-permute-start(f32[64,1152]{1,0:T(8,128)S(1)} %get-tuple-element.197), channel_id=1, source_target_pairs={{0,4},{4,8},{8,12},{12,0},{1,5},{5,9},{9,13},{13,1},{2,6},{6,10},{... | collective-permute-start | bytes 884744 | tf_op jit(solution)/shard_map/ppermute | solution.py:36
  377.4 16.2 %collective-permute-start.59 = (f32[384,1152]{1,0:T(8,128)S(1)}, f32[384,1152]{1,0:T(8,128)}, u32[]{:S(2)}, u32[]{:S(2)}) collective-permute-start(f32[384,1152]{1,0:T(8,128)S(1)} %constant_dynamic-update-slice_fusion.16), channel_id=1, source_target_pairs={{0,1},{1,0},{2,3},{3,2},{4,5},{5,4},{6,7},{7,6},{8,9},{9,8},{10,11... | collective-permute-start | bytes 5308424 | tf_op jit(solution)/shard_map/ppermute | solution.py:50
  387.8 37.9 %collective-permute-start.89 = (f32[4,144,576]{2,1,0:T(8,128)}, f32[4,144,576]{2,1,0:T(8,128)}, u32[]{:S(2)}, u32[]{:S(2)}) collective-permute-start(f32[4,144,576]{2,1,0:T(8,128)} %get-tuple-element.118), channel_id=1, source_target_pairs={{0,16},{16,0},{1,17},{17,1},{2,18},{18,2},{3,19},{19,3},{4,20},{20... | collective-permute-start | bytes 3981320 | tf_op jit(solution)/shard_map/ppermute | solution.py:54
  413.4 28.0 %collective-permute-start.61 = (f32[384,1152]{1,0:T(8,128)}, f32[384,1152]{1,0:T(8,128)}, u32[]{:S(2)}, u32[]{:S(2)}) collective-permute-start(f32[384,1152]{1,0:T(8,128)} %fusion.34), channel_id=1, source_target_pairs={{0,1},{1,0},{2,3},{3,2},{4,5},{5,4},{6,7},{7,6},{8,9},{9,8},{10,11... | collective-permute-start | bytes 5308424 | tf_op jit(solution)/shard_map/ppermute | solution.py:50
  415.6 13.7 %collective-permute-start.82 = (f32[504]{0:T(512)S(1)}, f32[504]{0:T(512)S(1)}, u32[]{:S(2)}, u32[]{:S(2)}) collective-permute-start(f32[504]{0:T(512)S(1)} %pad_maximum_fusion.48), channel_id=1, source_target_pairs={{0,12},{4,0},{8,4},{12,8},{1,13},{5,1},{9,5},{13,9},{2,14},{6,2},{... | collective-permute-start | bytes 6056 | tf_op jit(solution)/shard_map/ppermute | solution.py:36
  423.5 14.0 %collective-permute-start.67 = (f32[64,1152]{1,0:T(8,128)S(1)}, f32[64,1152]{1,0:T(8,128)S(1)}, u32[]{:S(2)}, u32[]{:S(2)}) collective-permute-start(f32[64,1152]{1,0:T(8,128)S(1)} %slice.567), channel_id=1, source_target_pairs={{0,2},{1,3},{2,0},{3,1},{4,6},{5,7},{6,4},{7,5},{8,10},{9,11},{10,... | collective-permute-start | bytes 884744 | tf_op jit(solution)/shard_map/ppermute | solution.py:46
  438.2 21.1 %collective-permute-start.68 = (f32[64,1152]{1,0:T(8,128)}, f32[64,1152]{1,0:T(8,128)}, u32[]{:S(2)}, u32[]{:S(2)}) collective-permute-start(f32[64,1152]{1,0:T(8,128)} %slice_add_fusion), channel_id=1, source_target_pairs={{0,12},{4,0},{8,4},{12,8},{1,13},{5,1},{9,5},{13,9},{2,14},{6,2},{... | collective-permute-start | bytes 884744 | tf_op jit(solution)/shard_map/ppermute | solution.py:36
  444.8 21.1 %collective-permute-start.90 = (f32[144,576]{1,0:T(8,128)}, f32[144,576]{1,0:T(8,128)}, u32[]{:S(2)}, u32[]{:S(2)}) collective-permute-start(f32[144,576]{1,0:T(8,128)} %get-tuple-element.122), channel_id=1, source_target_pairs={{0,4},{4,8},{8,12},{12,0},{1,5},{5,9},{9,13},{13,1},{2,6},{6,10},{... | collective-permute-start | bytes 995336 | tf_op jit(solution)/shard_map/ppermute | solution.py:36
  444.8 38.8 %collective-permute-start.91 = (f32[144,576]{1,0:T(8,128)}, f32[144,576]{1,0:T(8,128)}, u32[]{:S(2)}, u32[]{:S(2)}) collective-permute-start(f32[144,576]{1,0:T(8,128)} %get-tuple-element.123), channel_id=1, source_target_pairs={{0,8},{4,12},{8,0},{12,4},{1,9},{5,13},{9,1},{13,5},{2,10},{6,14},... | collective-permute-start | bytes 995336 | tf_op jit(solution)/shard_map/ppermute | solution.py:36
  447.1 14.7 %collective-permute-start.65 = (f32[64,1152]{1,0:T(8,128)}, f32[64,1152]{1,0:T(8,128)}, u32[]{:S(2)}, u32[]{:S(2)}) collective-permute-start(f32[64,1152]{1,0:T(8,128)} %get-tuple-element.243), channel_id=1, source_target_pairs={{0,2},{1,3},{2,0},{3,1},{4,6},{5,7},{6,4},{7,5},{8,10},{9,11},{10,... | collective-permute-start | bytes 884744 | tf_op jit(solution)/shard_map/ppermute | solution.py:46
  447.6 14.7 %collective-permute-start.63 = (f32[64,1152]{1,0:T(8,128)}, f32[64,1152]{1,0:T(8,128)}, u32[]{:S(2)}, u32[]{:S(2)}) collective-permute-start(f32[64,1152]{1,0:T(8,128)} %get-tuple-element.244), channel_id=1, source_target_pairs={{0,2},{1,3},{2,0},{3,1},{4,6},{5,7},{6,4},{7,5},{8,10},{9,11},{10,... | collective-permute-start | bytes 884744 | tf_op jit(solution)/shard_map/ppermute | solution.py:46
  459.3 42.6 %collective-permute-start.92 = (f32[144,576]{1,0:T(8,128)}, f32[144,576]{1,0:T(8,128)}, u32[]{:S(2)}, u32[]{:S(2)}) collective-permute-start(f32[144,576]{1,0:T(8,128)} %get-tuple-element.124), channel_id=1, source_target_pairs={{0,12},{4,0},{8,4},{12,8},{1,13},{5,1},{9,5},{13,9},{2,14},{6,2},{... | collective-permute-start | bytes 995336 | tf_op jit(solution)/shard_map/ppermute | solution.py:36
  461.8 43.0 %collective-permute-start.62 = (f32[64,1152]{1,0:T(8,128)}, f32[64,1152]{1,0:T(8,128)}, u32[]{:S(2)}, u32[]{:S(2)}) collective-permute-start(f32[64,1152]{1,0:T(8,128)} %get-tuple-element.242), channel_id=1, source_target_pairs={{0,2},{1,3},{2,0},{3,1},{4,6},{5,7},{6,4},{7,5},{8,10},{9,11},{10,... | collective-permute-start | bytes 884744 | tf_op jit(solution)/shard_map/ppermute | solution.py:46
  462.4 49.8 %collective-permute-start.84 = (f32[4,144,288]{2,1,0:T(8,128)}, f32[4,144,288]{2,1,0:T(8,128)}, u32[]{:S(2)}, u32[]{:S(2)}) collective-permute-start(f32[4,144,288]{2,1,0:T(8,128)} %dynamic-slice_bitcast_fusion.2), channel_id=1, source_target_pairs={{0,16},{16,0},{1,17},{17,1},{2,18},{18,2},{3,19},{19,3},{4,20},{20... | collective-permute-start | bytes 1990664 | tf_op jit(solution)/shard_map/ppermute | solution.py:54
  465.8 39.0 %collective-permute-start.69 = (f32[64,1152]{1,0:T(8,128)}, f32[64,1152]{1,0:T(8,128)}, u32[]{:S(2)}, u32[]{:S(2)}) collective-permute-start(f32[64,1152]{1,0:T(8,128)} %get-tuple-element.200), channel_id=1, source_target_pairs={{0,12},{4,0},{8,4},{12,8},{1,13},{5,1},{9,5},{13,9},{2,14},{6,2},{... | collective-permute-start | bytes 884744 | tf_op jit(solution)/shard_map/ppermute | solution.py:36
  483.7 26.5 %collective-permute-start.64 = (f32[64,1152]{1,0:T(8,128)}, f32[64,1152]{1,0:T(8,128)}, u32[]{:S(2)}, u32[]{:S(2)}) collective-permute-start(f32[64,1152]{1,0:T(8,128)} %get-tuple-element.245), channel_id=1, source_target_pairs={{0,4},{4,8},{8,12},{12,0},{1,5},{5,9},{9,13},{13,1},{2,6},{6,10},{... | collective-permute-start | bytes 884744 | tf_op jit(solution)/shard_map/ppermute | solution.py:36
  503.3 54.3 %collective-permute-start.93 = (f32[4,144,576]{2,1,0:T(8,128)S(1)}, f32[4,144,576]{2,1,0:T(8,128)S(1)}, u32[]{:S(2)}, u32[]{:S(2)}) collective-permute-start(f32[4,144,576]{2,1,0:T(8,128)S(1)} %pad_maximum_fusion.9), channel_id=1, source_target_pairs={{0,16},{16,0},{1,17},{17,1},{2,18},{18,2},{3,19},{19,3},{4,20},{20... | collective-permute-start | bytes 3981320 | tf_op jit(solution)/shard_map/ppermute | solution.py:54
  513.5 16.2 %collective-permute-start.86 = (f32[144,288]{1,0:T(8,128)S(1)}, f32[144,288]{1,0:T(8,128)S(1)}, u32[]{:S(2)}, u32[]{:S(2)}) collective-permute-start(f32[144,288]{1,0:T(8,128)S(1)} %get-tuple-element.298), channel_id=1, source_target_pairs={{0,8},{4,12},{8,0},{12,4},{1,9},{5,13},{9,1},{13,5},{2,10},{6,14},... | collective-permute-start | bytes 497672 | tf_op jit(solution)/shard_map/ppermute | solution.py:36
  513.6 16.1 %collective-permute-start.85 = (f32[144,288]{1,0:T(8,128)S(1)}, f32[144,288]{1,0:T(8,128)S(1)}, u32[]{:S(2)}, u32[]{:S(2)}) collective-permute-start(f32[144,288]{1,0:T(8,128)S(1)} %get-tuple-element.299), channel_id=1, source_target_pairs={{0,4},{4,8},{8,12},{12,0},{1,5},{5,9},{9,13},{13,1},{2,6},{6,10},{... | collective-permute-start | bytes 497672 | tf_op jit(solution)/shard_map/ppermute | solution.py:36
  515.9 15.4 %collective-permute-start.87 = (f32[144,288]{1,0:T(8,128)S(1)}, f32[144,288]{1,0:T(8,128)S(1)}, u32[]{:S(2)}, u32[]{:S(2)}) collective-permute-start(f32[144,288]{1,0:T(8,128)S(1)} %get-tuple-element.300), channel_id=1, source_target_pairs={{0,12},{4,0},{8,4},{12,8},{1,13},{5,1},{9,5},{13,9},{2,14},{6,2},{... | collective-permute-start | bytes 497672 | tf_op jit(solution)/shard_map/ppermute | solution.py:36
  531.3 25.0 %collective-permute-start.88 = (f32[4,144,288]{2,1,0:T(8,128)S(1)}, f32[4,144,288]{2,1,0:T(8,128)S(1)}, u32[]{:S(2)}, u32[]{:S(2)}) collective-permute-start(f32[4,144,288]{2,1,0:T(8,128)S(1)} %pad_maximum_fusion.19), channel_id=1, source_target_pairs={{0,16},{16,0},{1,17},{17,1},{2,18},{18,2},{3,19},{19,3},{4,20},{20... | collective-permute-start | bytes 1990664 | tf_op jit(solution)/shard_map/ppermute | solution.py:54
  576.1 43.3 %collective-permute-start.72 = (f32[64,576]{1,0:T(8,128)}, f32[64,576]{1,0:T(8,128)}, u32[]{:S(2)}, u32[]{:S(2)}) collective-permute-start(f32[64,576]{1,0:T(8,128)} %get-tuple-element.321), channel_id=1, source_target_pairs={{0,12},{4,0},{8,4},{12,8},{1,13},{5,1},{9,5},{13,9},{2,14},{6,2},{... | collective-permute-start | bytes 442376 | tf_op jit(solution)/shard_map/ppermute | solution.py:36
  576.1 43.3 %collective-permute-start.71 = (f32[64,576]{1,0:T(8,128)}, f32[64,576]{1,0:T(8,128)}, u32[]{:S(2)}, u32[]{:S(2)}) collective-permute-start(f32[64,576]{1,0:T(8,128)} %get-tuple-element.322), channel_id=1, source_target_pairs={{0,8},{4,12},{8,0},{12,4},{1,9},{5,13},{9,1},{13,5},{2,10},{6,14},... | collective-permute-start | bytes 442376 | tf_op jit(solution)/shard_map/ppermute | solution.py:36
  577.7 41.7 %collective-permute-start.70 = (f32[64,576]{1,0:T(8,128)}, f32[64,576]{1,0:T(8,128)}, u32[]{:S(2)}, u32[]{:S(2)}) collective-permute-start(f32[64,576]{1,0:T(8,128)} %get-tuple-element.323), channel_id=1, source_target_pairs={{0,4},{4,8},{8,12},{12,0},{1,5},{5,9},{9,13},{13,1},{2,6},{6,10},{... | collective-permute-start | bytes 442376 | tf_op jit(solution)/shard_map/ppermute | solution.py:36
  582.7 22.3 %collective-permute-start.77 = (f32[1,288]{1,0:T(1,128)}, f32[1,288]{1,0:T(1,128)}, u32[]{:S(2)}, u32[]{:S(2)}) collective-permute-start(f32[1,288]{1,0:T(1,128)} %broadcast_in_dim.39), channel_id=1, source_target_pairs={{0,4},{4,0},{8,12},{12,8},{1,5},{5,1},{9,13},{13,9},{2,6},{6,2},{1... | collective-permute-start | bytes 3464 | tf_op jit(solution)/shard_map/ppermute | solution.py:61
  588.5 33.9 %collective-permute-start.83 = (f32[4736]{0:T(1024)}, f32[4736]{0:T(1024)}, u32[]{:S(2)}, u32[]{:S(2)}) collective-permute-start(f32[4736]{0:T(1024)} %concatenate.162), channel_id=1, source_target_pairs={{0,16},{16,0},{1,17},{17,1},{2,18},{18,2},{3,19},{19,3},{4,20},{20... | collective-permute-start | bytes 56840 | tf_op jit(solution)/shard_map/ppermute | solution.py:54
  (131 other events, 1080.4 us)
Sparse Core Ops, SparseCore 0:
  99.7 75.9 all-gather.1
  387.9 108.1 reduce-scatter.1
